TPU v7x, 256 devices: a whole 4x4x8 slice. The times are simulated.
256 devices in a mesh: blk: 128 (over x, y, z), head: 2 (over core).
Axes of the slice: x: 4, y: 4, z: 8, core: 2. Of those that a mesh axis runs over, the one named last changes fastest.
Arguments:
- features: bfloat16 [131072, 512], P('blk')
- w_qkv: bfloat16 [3, 512, 512], P(None, None, 'head'), may hold values from -0.25 to 0.25
- w_out: bfloat16 [512, 512], P('head'), may hold values from -0.25 to 0.25
- key_lists: int32 [512, 16], P('blk'), may hold values from 0 to 511, as said below
- key_counts: int32 [512], P('blk'), may hold values from 2 to 16
- node_mask: int32 [131072], replicated, may hold values from 0 to 1, as said below
- hub_ids: int32 [8], replicated, may hold values from 0 to 511, as said below
Outputs:
- mixed: bfloat16 [131072, 512], P('blk', 'head')
Inputs may be any that keep to these rules, and one draw needn't show every extreme that they name: `key_lists`: in row b, entry 0 is b; entries 1 to 4 are positions in hub_ids (0 to 7); every other entry is a block within 2 blocks of b. `node_mask`: the first node of every block is 1. `hub_ids`: distinct block numbers.
All inputs are finite; a program needn't handle non-finite values.
Results may differ from a plain program's by a relative error of at most 0.0034.
The roundings to bfloat16 on the way count: a program that leaves them out, or rounds other values in their place, can miss the bound.
Values may be sent and summed in bfloat16 or wider, within the bound.
A program may use at most 64 MiB of HBM per device.

v0:
```python
import jax
import jax.numpy as jnp
from jax import lax
from jax.sharding import PartitionSpec as P

D = 512
HEADS = 8
REACH = 2
KL_HUB = 4


def with_halo(shard, sides, width):
    for axis, dim in sides:
        devices, length = (lax.axis_size(axis), shard.shape[dim])
        up = [(i, (i + 1) % devices) for i in range(devices - 1)]
        down = [(j, i) for i, j in up]
        last = lax.slice_in_dim(shard, length - width, length, axis=dim)
        leading = lax.slice_in_dim(shard, 0, width, axis=dim)
        before = lax.ppermute(last, axis, up)
        after = lax.ppermute(leading, axis, down)
        shard = jnp.concatenate([before, shard, after], axis=dim)
    return shard


def body(features, w_qkv, w_out, key_lists, key_counts, node_mask, hub_ids):
    rows, width = features.shape
    blocks_here = key_lists.shape[0]
    list_len = key_lists.shape[1]
    blk_rows = rows // blocks_here
    local = w_qkv.shape[2]
    head_size = D // HEADS
    heads_here = local // head_size
    hub_count = hub_ids.shape[0]
    scale = float(head_size) ** (-0.5)
    query = jnp.dot(features, w_qkv[0], preferred_element_type=jnp.float32).astype(jnp.bfloat16)
    keys = jnp.dot(features, w_qkv[1], preferred_element_type=jnp.float32).astype(jnp.bfloat16)
    values = jnp.dot(features, w_qkv[2], preferred_element_type=jnp.float32).astype(jnp.bfloat16)
    paired = jnp.concatenate([keys, values], axis=1)
    me = lax.axis_index("blk")
    first = me * blocks_here
    banded = with_halo(paired, (("blk", 0),), REACH * blk_rows)
    band_blocks = blocks_here + 2 * REACH
    banded = banded.reshape(band_blocks, blk_rows, 2 * local)
    mine = paired.reshape(blocks_here, blk_rows, 2 * local)
    owner = hub_ids // blocks_here
    slot_here = hub_ids % blocks_here
    picked = mine[slot_here].astype(jnp.float32)
    contrib = jnp.where((owner == me)[:, None, None], picked, jnp.zeros_like(picked))
    hubs = lax.psum(contrib, "blk").astype(jnp.bfloat16)
    pool = jnp.concatenate([banded, hubs], axis=0)
    masks = node_mask.reshape(node_mask.shape[0] // blk_rows, blk_rows)
    column = jnp.arange(list_len, dtype=jnp.int32)[None, :]
    is_hub = (column >= 1) & (column <= KL_HUB)
    slots = jnp.clip(key_lists, 0, hub_count - 1)
    target = jnp.where(is_hub, hub_ids[slots], key_lists)
    pool_index = jnp.where(is_hub, band_blocks + slots, key_lists - first + REACH)
    live = column < key_counts[:, None]
    valid = (masks[target] > 0) & live[:, :, None]
    query_blocks = query.reshape(blocks_here, blk_rows, heads_here, head_size)

    def one_block(operands):
        qrows, index, usable = operands
        taken = pool[index]
        block_keys = taken[:, :, :local].reshape(list_len * blk_rows, heads_here, head_size)
        block_vals = taken[:, :, local:].reshape(list_len * blk_rows, heads_here, head_size)
        usable = usable.reshape(list_len * blk_rows)
        score = (
            jnp.einsum("qhd,khd->hqk", qrows, block_keys, preferred_element_type=jnp.float32)
            * scale
        )
        score = jnp.where(usable[None, None, :], score, jnp.float32(-1e30))
        top = jnp.max(score, axis=2, keepdims=True)
        expo = jnp.where(usable[None, None, :], jnp.exp(score - top), jnp.float32(0.0))
        total = jnp.sum(expo, axis=2)
        weight = expo.astype(jnp.bfloat16)
        summed = jnp.einsum("hqk,khd->qhd", weight, block_vals, preferred_element_type=jnp.float32)
        attended = summed / jnp.transpose(total)[:, :, None]
        return attended.reshape(blk_rows, local).astype(jnp.bfloat16)

    attended = lax.map(one_block, (query_blocks, pool_index, valid)).reshape(rows, local)
    partial_out = jnp.dot(attended, w_out, preferred_element_type=jnp.float32)
    summed_out = lax.psum_scatter(partial_out, "head", scatter_dimension=1, tiled=True)
    share = width // lax.axis_size("head")
    resid = lax.dynamic_slice_in_dim(features, lax.axis_index("head") * share, share, 1)
    return (summed_out + resid.astype(jnp.float32)).astype(jnp.bfloat16)


def solution(mesh):
    placed = (
        P("blk", None),
        P(None, None, "head"),
        P("head", None),
        P("blk", None),
        P("blk"),
        P(),
        P(),
    )
    return jax.shard_map(
        body, mesh=mesh, in_specs=placed, out_specs=P("blk", "head"), check_vma=False
    )
```

profile of v0, /device:TPU:1, one launch (start us, length us, event | category | flops | bytes accessed | tf_op | source)
XLA Modules:
  0.0 949.8 jit_solution(18354718523766158233)
XLA Ops:
  6.5 1.8 convolution_convert_fusion.1
  8.4 1.9 convolution_convert_fusion.2
  11.5 5.2 collective-permute-start
  18.1 2.2 convolution_convert_fusion
  21.6 2.6 convert_select_fusion
  24.3 630.0 %all-reduce.1 = bf16[8,256,512]{2,1,0:T(8,128)(2,1)S(1)} all-reduce(f32[8,256,512]{2,1,0:T(8,128)} %convert_select_fusion), channel_id=1, replica_groups=mesh['blk'=128,'head'=2] {'blk'}, use_global_device_ids=true, to_apply=%region_0.1 | all-reduce | flops 1048576 | bytes 6291456 | tf_op jit(solution)/shard_map/psum | solution.py:49
  655.4 2.0 reshape.102
  657.5 2.7 reshape.144
  660.2 2.2 copy.17
  664.2 2.8 pad_maximum_fusion.1
  667.0 3.9 copy.19
  670.9 4.0 pad_maximum_fusion
  674.9 149.3 %while.10 = (s32[]{:T(128)}, bf16[4,256,256]{2,1,0:T(8,128)(2,1)S(1)}, s32[4,16]{1,0:T(4,128)S(1)}, bf16[16,256,512]{2,1,0:T(8,128)(2,1)}, pred[4,16,256]{2,1,0:...) while((s32[]{:T(128)}, bf16[4,256,256]{2,1,0:T(8,128)(2,1)S(1)}, s32[4,16]{1,0:T(4,128)S(1)}, ...), condition=%wide.region_4.5_spmd, body=%wide.region_1.4_spmd.sunk | while | flops 1099043840 | bytes 63738740 | solution.py:80
  674.9 5.0 gather_fusion
  679.9 4.6 fusion.75
  684.5 3.3 copy.29
  687.9 2.4 reshape.152
  690.2 9.7 %fusion.76 = (f32[4,256]{1,0:T(4,128)S(1)}, bf16[4,256,4096]{2,1,0:T(8,128)(2,1)}) fusion(pred[4096]{0:T(1024)(128)(4,1)S(1)} %broadcast_in_dim.96, bf16[4096,4,64]{0,2,1:T(8,128)(2,1)} %reshape.152, bf16[4,256,4,64]{1,3,2,0:T(8,128)(2,1)} %get-tuple-element.136, s32[]{:T(128)} %get-tuple-element.124), kind=kOutput, calls=%fused_computation.71.clone.1 | convolution fusion | flops 562040832 | bytes 10629632 | tf_op jit(solution)/shard_map/while/body/eval_jaxpr/sub | solution.py:73
  700.0 3.2 copy.28
  703.1 2.9 reshape.151
  706.0 6.0 fusion.77
  712.3 5.0 gather_fusion
  717.2 4.6 fusion.75
  721.8 3.3 copy.29
  725.2 2.4 reshape.152
  727.6 9.7 %fusion.76 = (f32[4,256]{1,0:T(4,128)S(1)}, bf16[4,256,4096]{2,1,0:T(8,128)(2,1)}) fusion(pred[4096]{0:T(1024)(128)(4,1)S(1)} %broadcast_in_dim.96, bf16[4096,4,64]{0,2,1:T(8,128)(2,1)} %reshape.152, bf16[4,256,4,64]{1,3,2,0:T(8,128)(2,1)} %get-tuple-element.136, s32[]{:T(128)} %get-tuple-element.124), kind=kOutput, calls=%fused_computation.71.clone.1 | convolution fusion | flops 562040832 | bytes 10629632 | tf_op jit(solution)/shard_map/while/body/eval_jaxpr/sub | solution.py:73
  737.3 3.2 copy.28
  740.5 2.9 reshape.151
  743.4 6.0 fusion.77
  749.6 5.0 gather_fusion
  754.5 4.6 fusion.75
  759.2 3.3 copy.29
  762.5 2.4 reshape.152
  764.9 9.7 %fusion.76 = (f32[4,256]{1,0:T(4,128)S(1)}, bf16[4,256,4096]{2,1,0:T(8,128)(2,1)}) fusion(pred[4096]{0:T(1024)(128)(4,1)S(1)} %broadcast_in_dim.96, bf16[4096,4,64]{0,2,1:T(8,128)(2,1)} %reshape.152, bf16[4,256,4,64]{1,3,2,0:T(8,128)(2,1)} %get-tuple-element.136, s32[]{:T(128)} %get-tuple-element.124), kind=kOutput, calls=%fused_computation.71.clone.1 | convolution fusion | flops 562040832 | bytes 10629632 | tf_op jit(solution)/shard_map/while/body/eval_jaxpr/sub | solution.py:73
  774.6 3.2 copy.28
  777.8 2.9 reshape.151
  780.7 6.0 fusion.77
  786.9 5.0 gather_fusion
  791.9 4.6 fusion.75
  796.5 3.3 copy.29
  799.8 2.4 reshape.152
  802.2 9.7 %fusion.76 = (f32[4,256]{1,0:T(4,128)S(1)}, bf16[4,256,4096]{2,1,0:T(8,128)(2,1)}) fusion(pred[4096]{0:T(1024)(128)(4,1)S(1)} %broadcast_in_dim.96, bf16[4096,4,64]{0,2,1:T(8,128)(2,1)} %reshape.152, bf16[4,256,4,64]{1,3,2,0:T(8,128)(2,1)} %get-tuple-element.136, s32[]{:T(128)} %get-tuple-element.124), kind=kOutput, calls=%fused_computation.71.clone.1 | convolution fusion | flops 562040832 | bytes 10629632 | tf_op jit(solution)/shard_map/while/body/eval_jaxpr/sub | solution.py:73
  811.9 3.2 copy.28
  815.1 2.9 reshape.151
  818.0 6.0 fusion.77
  824.2 1.8 fusion.52
  826.0 114.8 %reduce-scatter.2.cloned.1.call-done = f32[1024,256]{1,0:T(8,128)} async-done(((f32[1024,512]{1,0:T(8,128)}), f32[1024,256]{1,0:T(8,128)}) %reduce-scatter.2.cloned.1.call-update) | async-done | bytes 1048592 | tf_op jit(solution)/shard_map/reduce_scatter | solution.py:82
  940.8 2.2 add_convert_fusion
  (80 shorter events, 7.4 us)
Async XLA Ops:
  6.5 817.7 %copy-start = (bf16[256,512]{1,0:T(8,128)(2,1)S(1)}, bf16[256,512]{1,0:T(8,128)(2,1)}, u32[]{:S(2)}) copy-start(bf16[256,512]{1,0:T(8,128)(2,1)} %param.11) | copy-start | bytes 786436
  6.5 11.6 %copy-start.7 = (bf16[1024,512]{1,0:T(8,128)(2,1)S(1)}, bf16[1024,512]{1,0:T(8,128)(2,1)}, u32[]{:S(2)}) copy-start(bf16[1024,512]{1,0:T(8,128)(2,1)} %param.9) | copy-start | bytes 3145732
  6.5 934.3 %reduce-scatter.2.cloned.1.call-start = ((), (), s32[]{:S(2)}) async-start(), calls=%async_computation.1 | async-start | bytes 3145728 | tf_op jit(solution)/shard_map/reduce_scatter | solution.py:82
  8.4 9.6 %copy-start.3 = (bf16[1024,256]{0,1:T(8,128)(2,1)}, bf16[1024,256]{0,1:T(8,128)(2,1)S(1)}, u32[]{:S(2)}) copy-start(bf16[1024,256]{0,1:T(8,128)(2,1)S(1)} %convolution_convert_fusion.1) | copy-start | bytes 1572868
  10.4 7.7 copy-start.5
  10.4 10.5 %copy-start.1 = (s32[8]{0:T(128)S(1)}, s32[8]{0:T(128)}, u32[]{:S(2)}) copy-start(s32[8]{0:T(128)} %param.15) | copy-start | bytes 100
  11.5 652.7 %collective-permute-start = (bf16[512,512]{0,1:T(8,128)(2,1)}, bf16[512,512]{0,1:T(8,128)(2,1)}, u32[]{:S(2)}, u32[]{:S(2)}) collective-permute-start(bf16[512,512]{0,1:T(8,128)(2,1)} %get-tuple-element.66), channel_id=1, source_target_pairs={{0,2},{2,4},{4,6},{6,8},{8,10},{10,12},{12,14},{14,16},{16,18},{18... | collective-permute-start | bytes 1572872 | tf_op jit(solution)/shard_map/ppermute | solution.py:19
  16.7 647.5 %collective-permute-start.1 = (bf16[512,512]{0,1:T(8,128)(2,1)}, bf16[512,512]{0,1:T(8,128)(2,1)}, u32[]{:S(2)}, u32[]{:S(2)}) collective-permute-start(bf16[512,512]{0,1:T(8,128)(2,1)} %get-tuple-element.67), channel_id=1, source_target_pairs={{2,0},{4,2},{6,4},{8,6},{10,8},{12,10},{14,12},{16,14},{18,16},{20... | collective-permute-start | bytes 1572872 | tf_op jit(solution)/shard_map/ppermute | solution.py:20
  24.2 630.0 %copy-start.10 = (s32[4,16]{1,0:T(4,128)S(1)}, s32[4,16]{1,0:T(4,128)}, u32[]{:S(2)}) copy-start(s32[4,16]{1,0:T(4,128)} %param.12) | copy-start | bytes 772
  24.3 633.1 %copy-start.11 = (s32[4]{0:T(128)S(1)}, s32[4]{0:T(128)}, u32[]{:S(2)}) copy-start(s32[4]{0:T(128)} %param.13) | copy-start | bytes 52
  654.3 10.0 %copy-start.4 = (bf16[1024,256]{0,1:T(8,128)(2,1)S(1)}, bf16[1024,256]{0,1:T(8,128)(2,1)}, u32[]{:S(2)}) copy-start(bf16[1024,256]{0,1:T(8,128)(2,1)} %copy-done.3) | copy-start | bytes 1572868
  654.3 10.0 %copy-start.6 = (bf16[1024,256]{0,1:T(8,128)(2,1)S(1)}, bf16[1024,256]{0,1:T(8,128)(2,1)}, u32[]{:S(2)}) copy-start(bf16[1024,256]{0,1:T(8,128)(2,1)} %copy-done.5) | copy-start | bytes 1572868
  670.9 4.0 copy-start.9
  690.2 9.7 %copy-start.2 = (bf16[16,256,256]{2,1,0:T(8,128)(2,1)S(1)}, bf16[16,256,256]{2,1,0:T(8,128)(2,1)}, u32[]{:S(2)}) copy-start(bf16[16,256,256]{2,1,0:T(8,128)(2,1)} %get-tuple-element.113) | copy-start | bytes 6291460 | tf_op jit(solution)/shard_map/while
  727.6 9.7 %copy-start.2 = (bf16[16,256,256]{2,1,0:T(8,128)(2,1)S(1)}, bf16[16,256,256]{2,1,0:T(8,128)(2,1)}, u32[]{:S(2)}) copy-start(bf16[16,256,256]{2,1,0:T(8,128)(2,1)} %get-tuple-element.113) | copy-start | bytes 6291460 | tf_op jit(solution)/shard_map/while
  764.9 9.7 %copy-start.2 = (bf16[16,256,256]{2,1,0:T(8,128)(2,1)S(1)}, bf16[16,256,256]{2,1,0:T(8,128)(2,1)}, u32[]{:S(2)}) copy-start(bf16[16,256,256]{2,1,0:T(8,128)(2,1)} %get-tuple-element.113) | copy-start | bytes 6291460 | tf_op jit(solution)/shard_map/while
  802.2 9.7 %copy-start.2 = (bf16[16,256,256]{2,1,0:T(8,128)(2,1)S(1)}, bf16[16,256,256]{2,1,0:T(8,128)(2,1)}, u32[]{:S(2)}) copy-start(bf16[16,256,256]{2,1,0:T(8,128)(2,1)} %get-tuple-element.113) | copy-start | bytes 6291460 | tf_op jit(solution)/shard_map/while
  824.2 116.6 %copy-start.8 = (bf16[1024,512]{1,0:T(8,128)(2,1)S(1)}, bf16[1024,512]{1,0:T(8,128)(2,1)}, u32[]{:S(2)}) copy-start(bf16[1024,512]{1,0:T(8,128)(2,1)} %param.9) | copy-start | bytes 3145732
Sparse Core Ops, SparseCore 0:
  826.1 114.6 reduce-scatter.1
where the time goes:
time: 951 us; the launch traced here: 950 us
  blocking collectives  630 us (66%)
  waiting for transfers between devices  115 us (12%)
  local copies, waits for them, and re-layouts  101 us (11%)
  matrix products  70.8 us (7%)
  between operations  13.7 us (1%)
  other arithmetic  13.1 us (1%)
    psum x1, blocking collectives, body(): hubs = lax.psum(contrib, 'blk').astype(jnp.bfloat16)  630 us
    reduce_scatter x1, waiting for transfers between devices, body(): lax.psum_scatter(partial_out, 'head', scatter_dimension=1, tiled=True)  115 us
    sub x4, matrix products, one_block(): score - top  38.9 us
    slice x8, local copies, waits for them, and re-layouts, one_block(): taken[:, :, :local].reshape(list_len * blk_rows, heads_here, head_size)  31.9 us
    dot_general x4, matrix products, one_block(): jnp.einsum('hqk,khd->qhd', weight, block_vals, preferred_element_type=jnp...  24.2 us
    gather x4, local copies, waits for them, and re-layouts, one_block(): taken = pool[index]  19.8 us
  transfers between devices with their start and end apart: 3, of which 1 were waited for; matrix products, arithmetic and copies ran while one was open for 2% of the time, Pallas kernels for 0%

commit v1 on v0

v1 whole, which is shorter than its diff:
```python
import functools

import jax
import jax.numpy as jnp
from jax import lax
from jax.experimental import pallas as pl
from jax.experimental.pallas import tpu as pltpu
from jax.sharding import PartitionSpec as P

F32 = jnp.float32
BF16 = jnp.bfloat16
HEADS_HERE, DH, B = 4, 64, 256
NT = (((1,), (1,)), ((), ()))
LIMIT = 2.0e5
NEG = -1e30


def attn_kernel(mode, first_of, lists, counts, hub_ids, feat, hubs, halo, w_qkv, mask, out,
                qpad, keys, vals, bias, acc, top, att_t, cnt):
    first = first_of() * 4
    for b in range(4):
        for i in range(16):
            cnt[b, i] = 0
    for b in range(4):
        for j in range(16):
            entry = lists[b, j]
            if 1 <= j <= 4:
                at = 8 + entry
            else:
                at = entry - first + 2
            cnt[b, at] += jnp.where(j < counts[b], 1, 0)

    wq, wk = w_qkv[0], w_qkv[1]
    wv_t = w_qkv[2].T
    lane_head = lax.broadcasted_iota(jnp.int32, (256, 256), 1) // DH
    sums = (lax.broadcasted_iota(jnp.int32, (256, 128), 0) // DH
            == lax.broadcasted_iota(jnp.int32, (256, 128), 1)).astype(BF16)

    def most(rows):
        sq = rows.astype(F32)
        sq = (sq * sq).astype(BF16)
        return jnp.max(jnp.dot(sq, sums, preferred_element_type=F32), axis=0, keepdims=True)

    qn = jnp.zeros((1, 128), F32)
    for b in range(4):
        q = jnp.dot(feat[b * B:(b + 1) * B, :], wq, preferred_element_type=F32).astype(BF16)
        qn = jnp.maximum(qn, most(q))
        q = q * jnp.asarray(DH ** -0.5, BF16)
        for h in range(HEADS_HERE):
            qpad[b, h * B:(h + 1) * B, :] = jnp.where(lane_head == h, q, jnp.zeros_like(q))

    def block_rows(i):
        if i < 2:
            return halo[0, 0, i], halo[1, 0, i]
        if i < 6:
            own = feat[(i - 2) * B:(i - 1) * B, :]
            return own[:, :256], own[:, 256:]
        if i < 8:
            return halo[0, 1, i - 6], halo[1, 1, i - 6]
        k = i - 8
        left = jnp.concatenate([hubs[0, x, y, k] for x in range(4) for y in range(4)], axis=0)
        right = jnp.concatenate([hubs[1, y, x, k] for x in range(4) for y in range(4)], axis=0)
        return left, right

    kn = jnp.zeros((1, 128), F32)
    for i in range(16):
        r0, r1 = block_rows(i)
        if i < 2 or 6 <= i < 8:
            r0 = r0.reshape(B, 256)
            r1 = r1.reshape(B, 256)
        rows = jnp.concatenate([r0, r1], axis=1)
        k = jnp.dot(rows, wk, preferred_element_type=F32).astype(BF16)
        keys[i] = k
        kn = jnp.maximum(kn, most(k))
        if i < 8:
            node = jnp.clip(first + (i - 2), 0, mask.shape[0] - 1)
        else:
            node = hub_ids[i - 8]
        usable = mask[pl.ds(node, 1), :]
        usable = (usable > 0).astype(F32)
        v_t = lax.dot_general(wv_t, rows, NT, preferred_element_type=F32).astype(BF16)
        v_t = v_t * usable.astype(BF16)
        tail = jnp.concatenate([usable, jnp.zeros((15, 256), F32)], axis=0).astype(BF16)
        for h in range(HEADS_HERE):
            vals[i, h, 0:DH, :] = v_t[h * DH:(h + 1) * DH, :]
            vals[i, h, DH:DH + 16, :] = tail
        off = jnp.broadcast_to((usable - 1.0) * 1e30, (128, 256))
        bias[i] = off.T

    safe = jnp.max(qn) * jnp.max(kn) <= LIMIT

    def run(fast):
        @pl.loop(0, 4)
        def _(b):
            acc[...] = jnp.zeros_like(acc)
            if not fast:
                top[...] = jnp.full_like(top, NEG)

            @pl.loop(0, 13)
            def _(t):
                at = jnp.where(t < 5, b + t, t + 3)
                times = cnt[b, at]

                @pl.when(times > 0)
                def _():
                    scale = times.astype(F32)
                    kb = keys[at]
                    for h in range(HEADS_HERE):
                        s = lax.dot_general(kb, qpad[b, h * B:(h + 1) * B, :], NT,
                                            preferred_element_type=F32)
                        if fast:
                            p = jnp.exp(s).astype(BF16)
                            acc[h] += scale * jnp.dot(vals[at, h], p, preferred_element_type=F32)
                        else:
                            low = bias[at]
                            s = s + jnp.concatenate([low, low], axis=1)
                            old = top[h]
                            new = jnp.maximum(old, jnp.max(s, axis=0, keepdims=True))
                            top[h] = new
                            p = jnp.exp(s - new).astype(BF16)
                            acc[h] = jnp.exp(old - new) * acc[h] + scale * jnp.dot(
                                vals[at, h], p, preferred_element_type=F32)

            for h in range(HEADS_HERE):
                att_t[h * DH:(h + 1) * DH, :] = (acc[h, 0:DH, :] / acc[h, DH:DH + 1, :]).astype(BF16)
            out[pl.ds(pl.multiple_of(b * B, B), B), :] = att_t[...].T

    if mode == "both":
        @pl.when(safe)
        def _():
            run(True)

        @pl.when(jnp.logical_not(safe))
        def _():
            run(False)
    else:
        run(mode == "fast")


def attention(first_of, lists, counts, hub_ids, feat, hubs, halo, w_qkv, mask, mode="both"):
    smem = pl.BlockSpec(memory_space=pltpu.SMEM)
    vmem = pl.BlockSpec(memory_space=pltpu.VMEM)
    return pl.pallas_call(
        functools.partial(attn_kernel, mode, first_of),
        out_shape=jax.ShapeDtypeStruct((1024, 256), BF16),
        in_specs=[smem, smem, smem, vmem, vmem, vmem, vmem, vmem],
        out_specs=vmem,
        scratch_shapes=[
            pltpu.VMEM((4, 1024, 256), BF16),
            pltpu.VMEM((16, 256, 256), BF16),
            pltpu.VMEM((16, 4, 80, 256), BF16),
            pltpu.VMEM((16, 256, 128), F32),
            pltpu.VMEM((4, 80, 256), F32),
            pltpu.VMEM((4, 1, 256), F32),
            pltpu.VMEM((256, 256), BF16),
            pltpu.SMEM((4, 16), jnp.int32),
        ],
        compiler_params=pltpu.CompilerParams(vmem_limit_bytes=48 << 20),
        name="attention",
    )(lists, counts, hub_ids, feat, hubs, halo, w_qkv, mask)


MESH = pl.DeviceIdType.MESH


def comm_kernel(hub_ids, feat, hubs, halo, plane, zsend, zrecv, local,
                p_send, p_recv, z_send, z_recv, g_send, g_recv, a_send, a_recv,
                b_send, b_recv, c_send, c_recv, n_send, n_recv):
    me = lax.axis_index("blk")
    core = lax.axis_index("head")
    devices = lax.axis_size("blk")
    x, y, z = me // 32, (me // 8) % 4, me % 8
    a = jnp.where(core == 0, y, x)
    b = jnp.where(core == 0, x, y)
    step_a = jnp.where(core == 0, 8, 32)
    step_b = jnp.where(core == 0, 32, 8)
    columns = pl.ds(pl.multiple_of(core * 256, 256), 256)
    other = 1 - core
    after = (me + 1) % devices
    before = (me + devices - 1) % devices

    def at_plane(k):
        xx, yy = (x + k // 4) % 4, (y + k % 4) % 4
        return xx * 4 + yy, xx * 32 + yy * 8 + z

    def at_line(k):
        zz = (z + k) % 8
        return zz, x * 32 + y * 8 + zz

    def remote(src, dst, send, recv, blk, head):
        return pltpu.make_async_remote_copy(src_ref=src, dst_ref=dst, send_sem=send, recv_sem=recv,
                                            device_id=(blk, head), device_id_type=MESH)

    barrier = pltpu.get_barrier_semaphore()

    def greet(blk, head):
        pl.semaphore_signal(barrier, inc=1, device_id=(blk, head), device_id_type=MESH)

    for k in range(1, 16):
        greet(at_plane(k)[1], core)
    for k in range(1, 8):
        greet(at_line(k)[1], core)
    greet(me, other)
    greet(after, core)
    greet(before, core)
    mine = x * 4 + y
    own = pltpu.make_async_copy(feat.at[:, mine, :, columns], plane.at[mine], local)
    own.start()
    pl.semaphore_wait(barrier, 25)

    first = []
    for k in range(1, 16):
        part, blk = at_plane(k)
        first.append(remote(feat.at[:, part, :, columns], plane.at[mine],
                            p_send.at[k - 1], p_recv.at[k - 1], blk, core))
        first[-1].start()
    near = [
        remote(feat.at[2:4, :, :, columns], halo.at[core, 0], n_send.at[0], n_recv.at[0], after, core),
        remote(feat.at[0:2, :, :, columns], halo.at[core, 1], n_send.at[1], n_recv.at[1], before, core),
    ]
    for copy in near:
        copy.start()
    own.wait()
    for copy in first:
        copy.wait_recv()

    for k in range(8):
        h = hub_ids[k]
        zsend[k] = plane[lax.div(h, 32), lax.rem(h, 4)]
    second = []
    for k in range(1, 8):
        zz, blk = at_line(k)
        second.append(remote(zsend.at[zz], zrecv.at[z], z_send.at[k - 1], z_recv.at[k - 1], blk, core))
        second[-1].start()
    zrecv[z] = zsend[z]
    for copy in second:
        copy.wait_recv()

    hubs[core, b, a, z] = zrecv[lax.rem(lax.div(hub_ids[z], 4), 8)]
    third = []
    for k in range(1, 8):
        zz, blk = at_line(k)
        third.append(remote(hubs.at[core, b, a, z], hubs.at[core, b, a, z],
                            g_send.at[k - 1], g_recv.at[k - 1], blk, core))
        third[-1].start()
    for copy in third:
        copy.wait_recv()

    fourth = []
    for k in range(1, 4):
        fourth.append(remote(hubs.at[core, b, a], hubs.at[core, b, a], a_send.at[k - 1], a_recv.at[k - 1],
                             me + ((a + k) % 4 - a) * step_a, core))
        fourth[-1].start()
    for copy in fourth:
        copy.wait_recv()

    up, down, far = (b + 1) % 4, (b + 3) % 4, (b + 2) % 4
    up_blk = me + (up - b) * step_b
    down_blk = me + (down - b) * step_b

    def slab(i, n):
        return remote(hubs.at[core, i], hubs.at[core, i], c_send.at[n], c_recv.at[n], me, other)

    fifth = [
        remote(hubs.at[core, b], hubs.at[core, b], b_send.at[0], b_recv.at[0], up_blk, core),
        remote(hubs.at[core, b], hubs.at[core, b], b_send.at[1], b_recv.at[1], down_blk, core),
    ]
    for copy in fifth:
        copy.start()
    pair = [slab(b, 0)]
    pair[0].start()
    fifth[0].wait_recv()
    fifth.append(remote(hubs.at[core, down, 0:2], hubs.at[core, down, 0:2], b_send.at[2], b_recv.at[2],
                        up_blk, core))
    fifth[2].start()
    fifth[1].wait_recv()
    fifth.append(remote(hubs.at[core, up, 2:4], hubs.at[core, up, 2:4], b_send.at[3], b_recv.at[3],
                        down_blk, core))
    fifth[3].start()
    pair.append(slab(down, 1))
    pair[1].start()
    pair.append(slab(up, 2))
    pair[2].start()
    for i in range(2):
        near[i].wait_recv()
        pair.append(remote(halo.at[core, i], halo.at[core, i], c_send.at[4 + i], c_recv.at[4 + i], me, other))
        pair[-1].start()
    fifth[2].wait_recv()
    fifth[3].wait_recv()
    pair.append(slab(far, 3))
    pair[-1].start()

    for copy in first + near + second + third + fourth + fifth:
        copy.wait_send()
    for copy in pair:
        copy.wait()


def exchange(hub_ids, feat):
    dma = pltpu.SemaphoreType.DMA
    return pl.pallas_call(
        comm_kernel,
        out_shape=(jax.ShapeDtypeStruct((2, 4, 4, 8, 16, 256), BF16),
                   jax.ShapeDtypeStruct((2, 2, 2, 16, 16, 256), BF16)),
        in_specs=[pl.BlockSpec(memory_space=pltpu.SMEM), pl.BlockSpec(memory_space=pltpu.VMEM)],
        out_specs=(pl.BlockSpec(memory_space=pltpu.VMEM), pl.BlockSpec(memory_space=pltpu.VMEM)),
        scratch_shapes=[
            pltpu.VMEM((16, 4, 16, 256), BF16),
            pltpu.VMEM((8, 16, 256), BF16),
            pltpu.VMEM((8, 16, 256), BF16),
            dma(()),
            dma((15,)), dma((15,)), dma((7,)), dma((7,)), dma((7,)), dma((7,)), dma((3,)), dma((3,)),
            dma((4,)), dma((4,)), dma((6,)), dma((6,)), dma((2,)), dma((2,)),
        ],
        compiler_params=pltpu.CompilerParams(collective_id=0, has_side_effects=True,
                                             vmem_limit_bytes=32 << 20),
        name="exchange",
    )(hub_ids, feat.reshape(4, 16, 16, 512))


def body(features, w_qkv, w_out, key_lists, key_counts, node_mask, hub_ids):
    rows, width = features.shape
    local = w_qkv.shape[2]
    me = lax.axis_index("head")
    swap = [(0, 1), (1, 0)]
    share = width // 2
    w_mine = lax.dynamic_slice_in_dim(w_out, me * share, share, 1)
    w_sent = lax.dynamic_slice_in_dim(w_out, (1 - me) * share, share, 1)
    w_got = lax.ppermute(w_sent, "head", swap)
    hubs, halo = exchange(hub_ids, features)
    attended = attention(lambda: lax.axis_index("blk"), key_lists, key_counts, hub_ids, features,
                         hubs, halo, w_qkv, node_mask.reshape(-1, B))
    theirs = lax.ppermute(attended, "head", swap)
    resid = lax.dynamic_slice_in_dim(features, me * share, share, 1)
    mixed = (jnp.dot(attended, w_mine, preferred_element_type=F32)
             + jnp.dot(theirs, w_got, preferred_element_type=F32) + resid.astype(F32))
    return mixed.astype(BF16)


def solution(mesh):
    placed = (P("blk", None), P(None, None, "head"), P("head", None), P("blk", None), P("blk"), P(), P())
    return jax.shard_map(body, mesh=mesh, in_specs=placed, out_specs=P("blk", "head"), check_vma=False)
```

time: 951 us -> 102 us (0.11)
  the two profiles are of different devices: /device:TPU:1 before, /device:TPU:17 now
where the time goes in v1:
time: 102 us; the launch traced here: 101 us
  Pallas kernels  93 us (91%)
  local copies, waits for them, and re-layouts  5.01 us (5%)
  matrix products  1.39 us (1%)
  waiting for transfers between devices  1.19 us (1%)
    pallas_call x1, Pallas kernels, exchange(): pl.pallas_call(comm_kernel, out_shape=(jax.ShapeDtypeStruct((2, 4, 4, 8,...  53.4 us
    pallas_call x1, Pallas kernels, attention(): pl.pallas_call(functools.partial(attn_kernel, mode, first_of), out_shape=...  39.6 us
    unnamed x16, local copies, waits for them, and re-layouts  3.7 us
  transfers between devices with their start and end apart: 2, of which 1 were waited for; matrix products, arithmetic and copies ran while one was open for 0% of the time, Pallas kernels for 0%

profile of v1, /device:TPU:17, one launch (start us, length us, event | category | flops | bytes accessed | tf_op | source)
XLA Modules:
  0.0 101.3 jit_solution(14561050088603476757)
XLA Ops:
  0.0 0.0 copy-start
  0.0 0.0 copy-start.6
  0.0 0.0 copy-start.2
  0.0 0.0 copy-start.7
  0.0 1.3 %reshape.7.mask = s32[512,256]{1,0:T(8,128)S(1)} reshape(s32[131072]{0:T(1024)} %param.12) | data formatting | bytes 1048576 | tf_op jit(solution)/shard_map/reshape | solution.py:332
  1.3 0.0 copy-start.1
  1.3 1.2 %copy-done.1 = bf16[1024,512]{1,0:T(8,128)(2,1)S(1)} copy-done((bf16[1024,512]{1,0:T(8,128)(2,1)S(1)}, bf16[1024,512]{1,0:T(8,128)(2,1)}, u32[]{:S(2)}) %copy-start.1) | copy-done | bytes 1048600
  2.6 0.0 copy-start.5
  2.6 0.7 copy-done.5
  3.2 53.4 %exchange.1 = (bf16[2,4,4,8,16,256]{5,4,3,2,1,0:T(8,128)(2,1)S(1)}, bf16[2,2,2,16,16,256]{5,4,3,2,1,0:T(8,128)(2,1)S(1)}) custom-call(s32[8]{0:T(128)S(1)} %copy-done.5, bf16[4,16,16,512]{3,2,1,0:T(8,128)(2,1)S(1)} %bitcast.4), custom_call_target="tpu_custom_call" | custom-call | tf_op jit(solution)/shard_map/exchange/pallas_call | solution.py:301
  56.6 0.0 copy-done.6
  56.6 0.0 copy-done.2
  56.6 0.0 copy-done.7
  56.6 0.0 copy-start.3
  56.6 1.1 %copy-done.3 = bf16[3,512,256]{2,1,0:T(8,128)(2,1)S(1)} copy-done((bf16[3,512,256]{2,1,0:T(8,128)(2,1)S(1)}, bf16[3,512,256]{2,1,0:T(8,128)(2,1)}, u32[]{:S(2)}) %copy-start.3) | copy-done | bytes 786456
  57.7 0.0 copy-start.4
  57.8 0.7 copy-done.4
  58.4 39.6 %attention.1 = bf16[1024,256]{1,0:T(8,128)(2,1)S(1)} custom-call(s32[4,16]{1,0:T(4,128)S(1)} %copy-done.4, s32[4]{0:T(128)S(1)} %copy-done.7, s32[8]{0:T(128)S(1)} %copy-done.6, bf16[1024,512]{1,0:T(8,128)(2,1)S(1)} %copy-done.2, bf16[2,4,4,8,16,256]{5,4,3,2,1,0:T(8,128)(2,1)S(1)} %get-tuple-element.7.hubs, ...), custom_call_target="tpu_custom_call" | custom-call | tf_op jit(solution)/shard_map/attention/pallas_call | solution.py:143
  98.0 0.2 collective-permute-start
  98.3 0.0 copy-done
  98.3 0.5 collective-permute-start.1
  98.7 0.3 fusion.2
  99.0 1.2 %collective-permute-done.1 = bf16[256,256]{1,0:T(8,128)(2,1)S(1)} collective-permute-done((bf16[256,256]{1,0:T(8,128)(2,1)S(1)}, bf16[256,256]{1,0:T(8,128)(2,1)S(1)}, u32[]{:S(2)}, u32[]{:S(2)}) %collective-permute-start.1) | collective-permute-done | bytes 131104 | tf_op jit(solution)/shard_map/ppermute | solution.py:329
  100.2 0.0 collective-permute-done
  100.2 1.1 %fusion.1 = bf16[1024,256]{1,0:T(8,128)(2,1)} fusion(f32[1024,256]{1,0:T(8,128)S(1)} %fusion.2, bf16[1024,256]{1,0:T(8,128)(2,1)S(1)} %collective-permute-done, bf16[256,256]{1,0:T(8,128)(2,1)S(1)} %collective-permute-done.1, bf16[1024,512]{1,0:T(8,128)(2,1)S(1)} %copy-done.2, s32[]{:T(128)S(6)} %select_n.7), kind=kOutput, calls=%fused_computation.2 | convolution fusion | flops 135266304 | bytes 2752516 | tf_op jit(solution)/shard_map/dot_general | solution.py:336
  (1 shorter events, 0.0 us)
Async XLA Ops:
  0.0 98.3 %copy-start = (bf16[256,512]{1,0:T(8,128)(2,1)S(1)}, bf16[256,512]{1,0:T(8,128)(2,1)}, u32[]{:S(2)}) copy-start(bf16[256,512]{1,0:T(8,128)(2,1)} %param.9) | copy-start | bytes 786436
  0.0 56.6 %copy-start.6 = (s32[8]{0:T(128)S(1)}, s32[8]{0:T(128)}, u32[]{:S(2)}) copy-start(s32[8]{0:T(128)} %hub_ids.3) | copy-start | bytes 100
  0.0 56.6 %copy-start.2 = (bf16[1024,512]{1,0:T(8,128)(2,1)S(1)}, bf16[1024,512]{1,0:T(8,128)(2,1)}, u32[]{:S(2)}) copy-start(bf16[1024,512]{1,0:T(8,128)(2,1)} %feat.1) | copy-start | bytes 3145732
  0.0 56.6 %copy-start.7 = (s32[4]{0:T(128)S(1)}, s32[4]{0:T(128)}, u32[]{:S(2)}) copy-start(s32[4]{0:T(128)} %counts.1) | copy-start | bytes 52
  1.3 1.2 %copy-start.1 = (bf16[1024,512]{1,0:T(8,128)(2,1)S(1)}, bf16[1024,512]{1,0:T(8,128)(2,1)}, u32[]{:S(2)}) copy-start(bf16[1024,512]{1,0:T(8,128)(2,1)} %feat.1) | copy-start | bytes 3145732
  2.6 0.7 copy-start.5
  56.6 1.1 %copy-start.3 = (bf16[3,512,256]{2,1,0:T(8,128)(2,1)S(1)}, bf16[3,512,256]{2,1,0:T(8,128)(2,1)}, u32[]{:S(2)}) copy-start(bf16[3,512,256]{2,1,0:T(8,128)(2,1)} %w_qkv.1) | copy-start | bytes 2359300
  57.7 0.7 copy-start.4
  98.0 2.2 %collective-permute-start = (bf16[1024,256]{1,0:T(8,128)(2,1)S(1)}, bf16[1024,256]{1,0:T(8,128)(2,1)S(1)}, u32[]{:S(2)}, u32[]{:S(2)}) collective-permute-start(bf16[1024,256]{1,0:T(8,128)(2,1)S(1)} %attention.1), channel_id=1, source_target_pairs={{0,1},{1,0},{2,3},{3,2},{4,5},{5,4},{6,7},{7,6},{8,9},{9,8},{10,11... | collective-permute-start | bytes 1572872 | tf_op jit(solution)/shard_map/ppermute | solution.py:333
  98.3 1.9 %collective-permute-start.1 = (bf16[256,256]{1,0:T(8,128)(2,1)S(1)}, bf16[256,256]{1,0:T(8,128)(2,1)S(1)}, u32[]{:S(2)}, u32[]{:S(2)}) collective-permute-start(bf16[256,256]{1,0:T(8,128)(2,1)S(1)} %constant_dynamic-slice_fusion), channel_id=1, source_target_pairs={{0,1},{1,0},{2,3},{3,2},{4,5},{5,4},{6,7},{7,6},{8,9},{9,8},{10,11... | collective-permute-start | bytes 393224 | tf_op jit(solution)/shard_map/ppermute | solution.py:329

commit v2 on v0

v2 whole, which is shorter than its diff:
```python
import functools

import jax
import jax.numpy as jnp
from jax import lax
from jax.experimental import pallas as pl
from jax.experimental.pallas import tpu as pltpu
from jax.sharding import PartitionSpec as P

F32 = jnp.float32
BF16 = jnp.bfloat16
HEADS_HERE, DH, B = 4, 64, 256
TALL = DH + 16
NT = (((1,), (1,)), ((), ()))
NEG = -1e30
MESH = pl.DeviceIdType.MESH
VMEM = pl.BlockSpec(memory_space=pltpu.VMEM)
SMEM = pl.BlockSpec(memory_space=pltpu.SMEM)
ORDER = sorted(range(1, 16), key=lambda k: -(min(k // 4, 4 - k // 4) + min(k % 4, 4 - k % 4)))


def project(rows, wk, wv_t, usable, keys, vals, bias, i):
    keys[i] = jnp.dot(rows, wk, preferred_element_type=F32).astype(BF16)
    v_t = lax.dot_general(wv_t, rows, NT, preferred_element_type=F32).astype(BF16)
    tail = jnp.concatenate([usable, jnp.zeros((TALL - DH - 1, B), F32)], axis=0).astype(BF16)
    for h in range(HEADS_HERE):
        vals[i, h, 0:DH, :] = v_t[h * DH:(h + 1) * DH, :] * usable.astype(BF16)
        vals[i, h, DH:TALL, :] = tail
    bias[i] = jnp.broadcast_to((usable - 1.0) * 1e30, (128, B)).T


def attend(q_t, b, kb, vb, low, times, acc, top):
    low = low + jnp.where(times > 0, 0.0, NEG)
    low = jnp.concatenate([low, low], axis=1)
    scale = times.astype(F32)
    heads = range(HEADS_HERE)
    ss = [jnp.dot(kb, q_t[b, h], preferred_element_type=F32) for h in heads]
    ss = [s + low for s in ss]
    olds = [top[b, h] for h in heads]
    news = [jnp.maximum(o, jnp.max(s, axis=0, keepdims=True)) for o, s in zip(olds, ss)]
    ps = [jnp.exp(s - n).astype(BF16) for s, n in zip(ss, news)]
    got = [jnp.dot(vb[h], ps[h], preferred_element_type=F32) for h in heads]
    for h in heads:
        acc[b, h] = jnp.exp(olds[h] - news[h]) * acc[b, h] + scale * got[h]
        top[b, h] = news[h]


def near_kernel(hub_ids, lists, counts, feat, w_qkv, mask, hubs, q_t, acc, top,
                halo, plane, zsend, zrecv, wv_t, keys, vals, bias, local,
                p_send, p_recv, z_send, z_recv, g_send, g_recv, a_send, a_recv,
                c_send, c_recv, n_send, n_recv, m_send, m_recv):
    me = lax.axis_index("blk")
    core = lax.axis_index("head")
    devices = lax.axis_size("blk")
    x, y, z = me // 32, (me // 8) % 4, me % 8
    mine = x * 4 + y
    columns = pl.ds(pl.multiple_of(core * 256, 256), 256)
    other = 1 - core
    after = (me + 1) % devices
    before = (me + devices - 1) % devices

    def at_plane(k, sign=1):
        xx, yy = (x + sign * (k // 4) + 4) % 4, (y + sign * (k % 4) + 4) % 4
        return xx * 4 + yy, xx * 32 + yy * 8 + z

    def at_line(k):
        zz = (z + k) % 8
        return zz, x * 32 + y * 8 + zz

    def remote(src, dst, send, recv, blk, head):
        return pltpu.make_async_remote_copy(src_ref=src, dst_ref=dst, send_sem=send, recv_sem=recv,
                                            device_id=(blk, head), device_id_type=MESH)

    barrier = pltpu.get_barrier_semaphore()

    def greet(blk, head):
        pl.semaphore_signal(barrier, inc=1, device_id=(blk, head), device_id_type=MESH)

    for k in ORDER:
        greet(at_plane(k)[1], core)
    for k in range(1, 8):
        greet(at_line(k)[1], core)
    greet(after, core)
    greet(before, core)
    greet(me, other)
    own = pltpu.make_async_copy(feat.at[:, mine, :, columns], plane.at[mine], local)
    own.start()

    first = me * 4
    wv_t[...] = w_qkv[2].T
    row_head = lax.broadcasted_iota(jnp.int32, (B, B), 0) // DH
    acc[...] = jnp.zeros_like(acc)
    top[...] = jnp.full_like(top, NEG)

    def usable_of(node):
        return (mask[pl.ds(node, 1), :] > 0).astype(F32)

    @pl.loop(0, 4)
    def _(b):
        rows = feat[b].reshape(B, 512)
        q = jnp.dot(rows, w_qkv[0], preferred_element_type=F32).astype(BF16)
        q = (q * jnp.asarray(DH ** -0.5, BF16)).T
        for h in range(HEADS_HERE):
            q_t[b, h] = jnp.where(row_head == h, q, jnp.zeros_like(q))
        project(rows, w_qkv[1], wv_t[...], usable_of(first + b), keys, vals, bias, b + 2)

    def meet(b, i):
        times = jnp.int32(0)
        for j in [0] + list(range(5, 16)):
            hit = (lists[b, j] == first + i - 2) & (j < counts[b])
            times = times + jnp.where(hit, 1, 0)
        attend(q_t, b, keys[i], vals.at[i], bias[i], times, acc, top)

    pl.semaphore_wait(barrier, 25)

    scatter = {}
    for k in ORDER:
        part, blk = at_plane(k)
        scatter[k] = remote(feat.at[:, part, :, columns], plane.at[mine],
                            p_send.at[k - 1], p_recv.at[k - 1], blk, core)
        scatter[k].start()

    @pl.loop(0, 10)
    def _(n):
        b = (n + 1) // 3
        meet(b, b + 1 + (n + 1) % 3)

    own.wait()
    for copy in scatter.values():
        copy.wait_recv()

    for k in range(8):
        zsend[k] = plane[lax.div(hub_ids[k], 32), lax.rem(hub_ids[k], 4)]
    lines = []
    for k in (4, 3, 5, 2, 6, 1, 7):
        zz, blk = at_line(k)
        lines.append(remote(zsend.at[zz], zrecv.at[z], z_send.at[k - 1], z_recv.at[k - 1], blk, core))
        lines[-1].start()
    zrecv[z] = zsend[z]

    @pl.loop(0, 4)
    def _(n):
        b = (n % 2) * 2 + n // 2
        meet(b, (b + 2) % 4 + 2)

    for copy in lines:
        copy.wait_recv()
    hubs[core, mine, z] = zrecv[lax.rem(lax.div(hub_ids[z], 4), 8)]
    spread = []
    for k in (4, 3, 5, 2, 6, 1, 7):
        zz, blk = at_line(k)
        spread.append(remote(hubs.at[core, mine, z], hubs.at[core, mine, z],
                             g_send.at[k - 1], g_recv.at[k - 1], blk, core))
        spread[-1].start()
    for copy in spread:
        copy.wait_recv()

    gather = {}
    for k in ORDER:
        gather[k] = remote(hubs.at[core, mine], hubs.at[core, mine], a_send.at[k - 1], a_recv.at[k - 1],
                           at_plane(k)[1], core)
        gather[k].start()
    near = [
        remote(feat.at[2:4, :, :, columns], halo.at[core, 0], n_send.at[0], n_recv.at[0], after, core),
        remote(feat.at[0:2, :, :, columns], halo.at[core, 1], n_send.at[1], n_recv.at[1], before, core),
    ]
    for copy in near:
        copy.start()
    pair = [remote(hubs.at[core, mine], hubs.at[core, mine], c_send.at[0], c_recv.at[0], me, other)]
    pair[0].start()
    twin = []
    for i in range(2):
        near[i].wait_recv()
        twin.append(remote(halo.at[core, i], halo.at[core, i], m_send.at[i], m_recv.at[i], me, other))
        twin[i].start()
    for i in range(2):
        twin[i].wait()

    @pl.loop(0, 4)
    def _(n):
        side, at = n // 2, n % 2
        rows = jnp.concatenate([halo[0, side, at].reshape(B, 256), halo[1, side, at].reshape(B, 256)], axis=1)
        i = side * 6 + at
        node = (first + i - 2 + devices * 4) % (devices * 4)
        project(rows, w_qkv[1], wv_t[...], usable_of(node), keys, vals, bias, i)

    @pl.loop(0, 6)
    def _(n):
        meet(n // 2 + n // 3, (n + 1) // 2 + 4 * (n // 3))

    for k in ORDER:
        gather[k].wait_recv()
        part, _ = at_plane(k, -1)
        pair.append(remote(hubs.at[core, part], hubs.at[core, part], c_send.at[k], c_recv.at[k], me, other))
        pair[-1].start()
    for copy in pair:
        copy.wait()
    for copy in list(scatter.values()) + lines + spread + list(gather.values()) + near:
        copy.wait_send()


def near_attention(hub_ids, lists, counts, feat, w_qkv, mask):
    dma = pltpu.SemaphoreType.DMA
    return pl.pallas_call(
        near_kernel,
        out_shape=(jax.ShapeDtypeStruct((2, 16, 8, 16, 256), BF16),
                   jax.ShapeDtypeStruct((4, HEADS_HERE, B, B), BF16),
                   jax.ShapeDtypeStruct((4, HEADS_HERE, TALL, B), F32),
                   jax.ShapeDtypeStruct((4, HEADS_HERE, 1, B), F32)),
        in_specs=[SMEM, SMEM, SMEM, VMEM, VMEM, VMEM],
        out_specs=(VMEM, VMEM, VMEM, VMEM),
        scratch_shapes=[
            pltpu.VMEM((2, 2, 2, 16, 16, 256), BF16),
            pltpu.VMEM((16, 4, 16, 256), BF16),
            pltpu.VMEM((8, 16, 256), BF16),
            pltpu.VMEM((8, 16, 256), BF16),
            pltpu.VMEM((256, 512), BF16),
            pltpu.VMEM((8, B, B), BF16),
            pltpu.VMEM((8, HEADS_HERE, TALL, B), BF16),
            pltpu.VMEM((8, B, 128), F32),
            dma(()),
            dma((15,)), dma((15,)), dma((7,)), dma((7,)), dma((7,)), dma((7,)), dma((15,)), dma((15,)),
            dma((16,)), dma((16,)), dma((2,)), dma((2,)), dma((2,)), dma((2,)),
        ],
        compiler_params=pltpu.CompilerParams(collective_id=0, has_side_effects=True,
                                             vmem_limit_bytes=40 << 20),
        name="near",
    )(hub_ids, lists, counts, feat.reshape(4, 16, 16, 512), w_qkv, mask)


def hub_kernel(hub_ids, lists, counts, hubs, q_t, acc_in, top_in, w_qkv, mask, out,
               wv_t, keys, vals, bias, acc, top, att_t, cnt):
    for b in range(4):
        for i in range(8):
            cnt[b, i] = 0
        for j in range(1, 5):
            cnt[b, lists[b, j]] += jnp.where(j < counts[b], 1, 0)
    acc[...] = acc_in[...]
    top[...] = top_in[...]
    wv_t[...] = w_qkv[2].T

    @pl.loop(0, 8)
    def _(k):
        rows = jnp.concatenate([
            jnp.concatenate([hubs[c, p, k] for p in range(16)], axis=0) for c in range(2)], axis=1)
        usable = (mask[pl.ds(hub_ids[k], 1), :] > 0).astype(F32)
        project(rows, w_qkv[1], wv_t[...], usable, keys, vals, bias, k)

    @pl.loop(0, 4)
    def _(b):
        @pl.loop(0, 8)
        def _(k):
            times = cnt[b, k]

            @pl.when(times > 0)
            def _():
                attend(q_t, b, keys[k], vals.at[k], bias[k], times, acc, top)

        for h in range(HEADS_HERE):
            att_t[h * DH:(h + 1) * DH, :] = (acc[b, h, 0:DH, :] / acc[b, h, DH:DH + 1, :]).astype(BF16)
        out[pl.ds(pl.multiple_of(b * B, B), B), :] = att_t[...].T


def hub_attention(hub_ids, lists, counts, hubs, q_t, acc, top, w_qkv, mask):
    return pl.pallas_call(
        hub_kernel,
        out_shape=jax.ShapeDtypeStruct((1024, 256), BF16),
        in_specs=[SMEM, SMEM, SMEM] + [VMEM] * 6,
        out_specs=VMEM,
        scratch_shapes=[
            pltpu.VMEM((256, 512), BF16),
            pltpu.VMEM((8, B, B), BF16),
            pltpu.VMEM((8, HEADS_HERE, TALL, B), BF16),
            pltpu.VMEM((8, B, 128), F32),
            pltpu.VMEM((4, HEADS_HERE, TALL, B), F32),
            pltpu.VMEM((4, HEADS_HERE, 1, B), F32),
            pltpu.VMEM((B, B), BF16),
            pltpu.SMEM((4, 8), jnp.int32),
        ],
        compiler_params=pltpu.CompilerParams(vmem_limit_bytes=40 << 20),
        name="hub",
    )(hub_ids, lists, counts, hubs, q_t, acc, top, w_qkv, mask)


def body(features, w_qkv, w_out, key_lists, key_counts, node_mask, hub_ids):
    width = features.shape[1]
    me = lax.axis_index("head")
    swap = [(0, 1), (1, 0)]
    share = width // 2
    mask = node_mask.reshape(-1, B)
    w_mine = lax.dynamic_slice_in_dim(w_out, me * share, share, 1)
    w_sent = lax.dynamic_slice_in_dim(w_out, (1 - me) * share, share, 1)
    w_got = lax.ppermute(w_sent, "head", swap)
    hubs, q_t, acc, top = near_attention(hub_ids, key_lists, key_counts, features, w_qkv, mask)
    attended = hub_attention(hub_ids, key_lists, key_counts, hubs, q_t, acc, top, w_qkv, mask)
    theirs = lax.ppermute(attended, "head", swap)
    resid = lax.dynamic_slice_in_dim(features, me * share, share, 1)
    mixed = (jnp.dot(attended, w_mine, preferred_element_type=F32)
             + jnp.dot(theirs, w_got, preferred_element_type=F32) + resid.astype(F32))
    return mixed.astype(BF16)


def solution(mesh):
    placed = (P("blk", None), P(None, None, "head"), P("head", None), P("blk", None), P("blk"), P(), P())
    return jax.shard_map(body, mesh=mesh, in_specs=placed, out_specs=P("blk", "head"), check_vma=False)
```

time: 951 us -> 73.9 us (0.08)
  blocking collectives: 630 us -> 0 us
  waiting for transfers between devices: 115 us -> 1.19 us
  local copies, waits for them, and re-layouts: 101 us -> 5.65 us
  matrix products: 70.8 us -> 1.4 us
  Pallas kernels: 0 us -> 64.7 us
  between operations: 13.7 us -> 0.06 us
  other arithmetic: 13.1 us -> 0 us
    psum x1 -> x0, blocking collectives: 630 us -> none  [body(): hubs = lax.psum(contrib, 'blk').astype(jnp.bfloat16)]
    reduce_scatter x1 -> x0, waiting for transfers between devices: 115 us -> none  [body(): lax.psum_scatter(partial_out, 'head', scatter_dimension=1, tiled=True)]
    pallas_call x0 -> x2, Pallas kernels: none -> 64.7 us  [the longest x1 52.6 us: near_attention(): pl.pallas_call(near_kernel, out_shape=(jax.ShapeDtypeStruct((2, 16, 8, 16...]
    slice x12 -> x0, local copies, waits for them, and re-layouts: 44.6 us -> none  [the longest x8 31.9 us: one_block(): taken[:, :, :local].reshape(list_len * blk_rows, heads_here, head_size)]
    sub x4 -> x0, matrix products: 38.9 us -> none  [one_block(): score - top]
    dot_general x8 -> x2, matrix products: 31.9 us -> 1.4 us  [the longest x1 1.11 us: body(): jnp.dot(theirs, w_got, preferred_element_type=F32)]
    reshape x12 -> x1, local copies, waits for them, and re-layouts: 30.2 us -> 1.29 us  [body(): mask = node_mask.reshape(-1, B)]
    gather x8 -> x0, local copies, waits for them, and re-layouts: 23 us -> none  [the longest x4 19.8 us: one_block(): taken = pool[index]]
  transfers between devices with their start and end apart: 3 -> 2, of which waited for: 1 -> 1; matrix products, arithmetic and copies ran while one was open for 2% -> 0% of each run, Pallas kernels for 0% -> 0%
where the time goes in v2:
time: 73.9 us; the launch traced here: 73.7 us
  Pallas kernels  64.7 us (88%)
  local copies, waits for them, and re-layouts  5.65 us (8%)
  matrix products  1.4 us (2%)
  waiting for transfers between devices  1.19 us (2%)
    pallas_call x1, Pallas kernels, near_attention(): pl.pallas_call(near_kernel, out_shape=(jax.ShapeDtypeStruct((2, 16, 8, 16...  52.6 us
    pallas_call x1, Pallas kernels, hub_attention(): pl.pallas_call(hub_kernel, out_shape=jax.ShapeDtypeStruct((1024, 256), BF...  12.1 us
    unnamed x16, local copies, waits for them, and re-layouts  4.36 us
  transfers between devices with their start and end apart: 2, of which 1 were waited for; matrix products, arithmetic and copies ran while one was open for 0% of the time, Pallas kernels for 0%

profile of v2, /device:TPU:1, one launch (start us, length us, event | category | flops | bytes accessed | tf_op | source)
XLA Modules:
  0.0 73.7 jit_solution(16768286496684184004)
XLA Ops:
  0.0 0.0 copy-start
  0.0 0.0 copy-start.2
  0.0 1.3 %reshape.7.mask = s32[512,256]{1,0:T(8,128)S(1)} reshape(s32[131072]{0:T(1024)} %param.12) | data formatting | bytes 1048576 | tf_op jit(solution)/shard_map/reshape | solution.py:290
  1.3 0.0 copy-start.1
  1.3 1.1 %copy-done.1 = bf16[3,512,256]{2,1,0:T(8,128)(2,1)S(1)} copy-done((bf16[3,512,256]{2,1,0:T(8,128)(2,1)S(1)}, bf16[3,512,256]{2,1,0:T(8,128)(2,1)}, u32[]{:S(2)}) %copy-start.1) | copy-done | bytes 786456
  2.4 0.0 copy-start.3
  2.4 1.2 %copy-done.3 = bf16[1024,512]{1,0:T(8,128)(2,1)S(1)} copy-done((bf16[1024,512]{1,0:T(8,128)(2,1)S(1)}, bf16[1024,512]{1,0:T(8,128)(2,1)}, u32[]{:S(2)}) %copy-start.3) | copy-done | bytes 1048600
  3.7 0.0 copy-start.5
  3.7 0.7 copy-done.5
  4.3 0.0 copy-start.6
  4.3 0.7 copy-done.6
  5.0 0.0 copy-start.7
  5.0 0.7 copy-done.7
  5.7 52.6 %near.1 = (bf16[2,16,8,16,256]{4,3,2,1,0:T(8,128)(2,1)S(1)}, bf16[4,4,256,256]{3,2,1,0:T(8,128)(2,1)S(1)}, f32[4,4,80,256]{3,2,1,0:T(8,128)S(1)}, f32[4,4,1,256]{3,2,1,0:T(1,128)S(1)}) custom-call(s32[8]{0:T(128)S(1)} %copy-done.6, s32[4,16]{1,0:T(4,128)S(1)} %copy-done.5, s32[4]{0:T(128)S(1)} %copy-done.7, bf16[4,16,16,512]{3,2,1,0:T(8,128)(2,1)S(1)} %bitcast.4, ...), custom_call_target="tpu_custom_call" | custom-call | tf_op jit(solution)/shard_map/near/pallas_call | solution.py:204
  58.3 0.0 copy-done.2
  58.3 12.1 %hub.1 = bf16[1024,256]{1,0:T(8,128)(2,1)S(1)} custom-call(s32[8]{0:T(128)S(1)} %copy-done.6, s32[4,16]{1,0:T(4,128)S(1)} %copy-done.5, s32[4]{0:T(128)S(1)} %copy-done.7, bf16[2,16,8,16,256]{4,3,2,1,0:T(8,128)(2,1)S(1)} %get-tuple-element.9.hubs, bf16[4,4,256,256]{3,2,1,0:T(8,128)(2,1)S(1)} %get-tuple-element.10.q_t, ...), custom_call_target="tpu_custom_call" | custom-call | tf_op jit(solution)/shard_map/hub/pallas_call | solution.py:265
  70.4 0.0 copy-start.4
  70.4 0.5 collective-permute-start
  70.8 0.0 copy-done
  70.9 0.2 collective-permute-start.1
  71.1 0.3 fusion.2
  71.4 1.2 %collective-permute-done.1 = bf16[256,256]{1,0:T(8,128)(2,1)S(1)} collective-permute-done((bf16[256,256]{1,0:T(8,128)(2,1)S(1)}, bf16[256,256]{1,0:T(8,128)(2,1)S(1)}, u32[]{:S(2)}, u32[]{:S(2)}) %collective-permute-start.1) | collective-permute-done | bytes 131104 | tf_op jit(solution)/shard_map/ppermute | solution.py:293
  72.6 0.0 collective-permute-done
  72.6 0.0 copy-done.4
  72.6 1.1 %fusion.1 = bf16[1024,256]{1,0:T(8,128)(2,1)} fusion(f32[1024,256]{1,0:T(8,128)S(1)} %fusion.2, bf16[1024,256]{1,0:T(8,128)(2,1)S(1)} %collective-permute-done, bf16[256,256]{1,0:T(8,128)(2,1)S(1)} %collective-permute-done.1, bf16[1024,512]{1,0:T(8,128)(2,1)S(1)} %copy-done.4, s32[]{:T(128)S(6)} %select_n.7), kind=kOutput, calls=%fused_computation.2 | convolution fusion | flops 135266304 | bytes 2752516 | tf_op jit(solution)/shard_map/dot_general | solution.py:299
  (1 shorter events, 0.0 us)
Async XLA Ops:
  0.0 70.8 %copy-start = (bf16[256,512]{1,0:T(8,128)(2,1)S(1)}, bf16[256,512]{1,0:T(8,128)(2,1)}, u32[]{:S(2)}) copy-start(bf16[256,512]{1,0:T(8,128)(2,1)} %param.9) | copy-start | bytes 786436
  0.0 58.3 %copy-start.2 = (bf16[3,512,256]{2,1,0:T(8,128)(2,1)S(1)}, bf16[3,512,256]{2,1,0:T(8,128)(2,1)}, u32[]{:S(2)}) copy-start(bf16[3,512,256]{2,1,0:T(8,128)(2,1)} %w_qkv.3) | copy-start | bytes 2359300
  1.3 1.1 %copy-start.1 = (bf16[3,512,256]{2,1,0:T(8,128)(2,1)S(1)}, bf16[3,512,256]{2,1,0:T(8,128)(2,1)}, u32[]{:S(2)}) copy-start(bf16[3,512,256]{2,1,0:T(8,128)(2,1)} %w_qkv.3) | copy-start | bytes 2359300
  2.4 1.2 %copy-start.3 = (bf16[1024,512]{1,0:T(8,128)(2,1)S(1)}, bf16[1024,512]{1,0:T(8,128)(2,1)}, u32[]{:S(2)}) copy-start(bf16[1024,512]{1,0:T(8,128)(2,1)} %param.7) | copy-start | bytes 3145732
  3.7 0.7 copy-start.5
  4.3 0.7 copy-start.6
  5.0 0.7 copy-start.7
  70.4 2.2 %copy-start.4 = (bf16[1024,512]{1,0:T(8,128)(2,1)S(1)}, bf16[1024,512]{1,0:T(8,128)(2,1)}, u32[]{:S(2)}) copy-start(bf16[1024,512]{1,0:T(8,128)(2,1)} %param.7) | copy-start | bytes 3145732
  70.4 2.2 %collective-permute-start = (bf16[1024,256]{1,0:T(8,128)(2,1)S(1)}, bf16[1024,256]{1,0:T(8,128)(2,1)S(1)}, u32[]{:S(2)}, u32[]{:S(2)}) collective-permute-start(bf16[1024,256]{1,0:T(8,128)(2,1)S(1)} %hub.1), channel_id=1, source_target_pairs={{0,1},{1,0},{2,3},{3,2},{4,5},{5,4},{6,7},{7,6},{8,9},{9,8},{10,11... | collective-permute-start | bytes 1572872 | tf_op jit(solution)/shard_map/ppermute | solution.py:296
  70.9 1.7 %collective-permute-start.1 = (bf16[256,256]{1,0:T(8,128)(2,1)S(1)}, bf16[256,256]{1,0:T(8,128)(2,1)S(1)}, u32[]{:S(2)}, u32[]{:S(2)}) collective-permute-start(bf16[256,256]{1,0:T(8,128)(2,1)S(1)} %constant_dynamic-slice_fusion), channel_id=1, source_target_pairs={{0,1},{1,0},{2,3},{3,2},{4,5},{5,4},{6,7},{7,6},{8,9},{9,8},{10,11... | collective-permute-start | bytes 393224 | tf_op jit(solution)/shard_map/ppermute | solution.py:293

commit v3 on v2

--- a/solution.py
+++ b/solution.py
@@ -16,6 +16,7 @@
 MESH = pl.DeviceIdType.MESH
 VMEM = pl.BlockSpec(memory_space=pltpu.VMEM)
 SMEM = pl.BlockSpec(memory_space=pltpu.SMEM)
+HBM = pl.BlockSpec(memory_space=pltpu.HBM)
 ORDER = sorted(range(1, 16), key=lambda k: -(min(k // 4, 4 - k // 4) + min(k % 4, 4 - k % 4)))
 
 
@@ -45,9 +46,10 @@
         top[b, h] = news[h]
 
 
-def near_kernel(hub_ids, lists, counts, feat, w_qkv, mask, hubs, q_t, acc, top,
-                halo, plane, zsend, zrecv, wv_t, keys, vals, bias, local,
-                p_send, p_recv, z_send, z_recv, g_send, g_recv, a_send, a_recv,
+def near_kernel(hub_ids_at, lists_at, counts_at, feat_at, w_at, mask, hubs, q_t, acc, top,
+                hub_ids, lists, counts, feat, w_qkv, marks,
+                halo, plane, zsend, zrecv, wv_t, keys, vals, bias, local, mark_sem,
+                p_send, p_recv, z_send, z_recv, g_send, g_recv, a_send, a_recv, b_send, b_recv,
                 c_send, c_recv, n_send, n_recv, m_send, m_recv):
     me = lax.axis_index("blk")
     core = lax.axis_index("head")
@@ -83,17 +85,30 @@
     greet(after, core)
     greet(before, core)
     greet(me, other)
-    own = pltpu.make_async_copy(feat.at[:, mine, :, columns], plane.at[mine], local)
-    own.start()
-
+    own = pltpu.make_async_copy(feat_at.at[:, mine, :, columns], plane.at[mine], local.at[0])
+    loads = [pltpu.make_async_copy(w_at, w_qkv, local.at[1]),
+             pltpu.make_async_copy(feat_at, feat, local.at[2]),
+             pltpu.make_async_copy(hub_ids_at, hub_ids, local.at[3]),
+             pltpu.make_async_copy(lists_at, lists, local.at[4]),
+             pltpu.make_async_copy(counts_at, counts, local.at[5]),
+             own]
     first = me * 4
+    for i in range(8):
+        node = (first + i - 2 + devices * 4) % (devices * 4)
+        loads.append(pltpu.make_async_copy(mask.at[pl.ds(pl.multiple_of(node * B, B), B)], marks.at[i, 0],
+                                           mark_sem.at[i]))
+    for copy in loads:
+        copy.start()
+    for copy in loads:
+        copy.wait()
+
     wv_t[...] = w_qkv[2].T
     row_head = lax.broadcasted_iota(jnp.int32, (B, B), 0) // DH
     acc[...] = jnp.zeros_like(acc)
     top[...] = jnp.full_like(top, NEG)
 
-    def usable_of(node):
-        return (mask[pl.ds(node, 1), :] > 0).astype(F32)
+    def usable_of(i):
+        return (marks[i] > 0).astype(F32)
 
     @pl.loop(0, 4)
     def _(b):
@@ -102,7 +117,7 @@
         q = (q * jnp.asarray(DH ** -0.5, BF16)).T
         for h in range(HEADS_HERE):
             q_t[b, h] = jnp.where(row_head == h, q, jnp.zeros_like(q))
-        project(rows, w_qkv[1], wv_t[...], usable_of(first + b), keys, vals, bias, b + 2)
+        project(rows, w_qkv[1], wv_t[...], usable_of(b + 2), keys, vals, bias, b + 2)
 
     def meet(b, i):
         times = jnp.int32(0)
@@ -116,7 +131,7 @@
     scatter = {}
     for k in ORDER:
         part, blk = at_plane(k)
-        scatter[k] = remote(feat.at[:, part, :, columns], plane.at[mine],
+        scatter[k] = remote(feat_at.at[:, part, :, columns], plane.at[mine],
                             p_send.at[k - 1], p_recv.at[k - 1], blk, core)
         scatter[k].start()
 
@@ -125,7 +140,6 @@
         b = (n + 1) // 3
         meet(b, b + 1 + (n + 1) % 3)
 
-    own.wait()
     for copy in scatter.values():
         copy.wait_recv()
 
@@ -155,19 +169,42 @@
     for copy in spread:
         copy.wait_recv()
 
-    gather = {}
-    for k in ORDER:
-        gather[k] = remote(hubs.at[core, mine], hubs.at[core, mine], a_send.at[k - 1], a_recv.at[k - 1],
-                           at_plane(k)[1], core)
-        gather[k].start()
+    along = jnp.where(core == 0, y, x)
+    across = jnp.where(core == 0, x, y)
+    along_blk, across_blk = jnp.where(core == 0, 8, 32), jnp.where(core == 0, 32, 8)
+    along_part, across_part = jnp.where(core == 0, 1, 4), jnp.where(core == 0, 4, 1)
+
+    def part_of(da, db):
+        return ((along + da + 4) % 4) * along_part + ((across + db + 4) % 4) * across_part
+
+    def send_on(da):
+        part = part_of(-da, 0)
+        sent = []
+        for db in (2, 1, 3):
+            n = da * 3 + db - 1
+            sent.append(remote(hubs.at[core, part], hubs.at[core, part], b_send.at[n], b_recv.at[n],
+                               me + ((across + db) % 4 - across) * across_blk, core))
+            sent[-1].start()
+        pair.append(remote(hubs.at[core, part], hubs.at[core, part], c_send.at[da], c_recv.at[da], me, other))
+        pair[-1].start()
+        return sent
+
+    pair = []
+    gather = []
+    for da in (2, 1, 3):
+        gather.append(remote(hubs.at[core, mine], hubs.at[core, mine], a_send.at[da - 1], a_recv.at[da - 1],
+                             me + ((along + da) % 4 - along) * along_blk, core))
+        gather[-1].start()
+    onward = {0: send_on(0)}
     near = [
-        remote(feat.at[2:4, :, :, columns], halo.at[core, 0], n_send.at[0], n_recv.at[0], after, core),
-        remote(feat.at[0:2, :, :, columns], halo.at[core, 1], n_send.at[1], n_recv.at[1], before, core),
+        remote(feat_at.at[2:4, :, :, columns], halo.at[core, 0], n_send.at[0], n_recv.at[0], after, core),
+        remote(feat_at.at[0:2, :, :, columns], halo.at[core, 1], n_send.at[1], n_recv.at[1], before, core),
     ]
     for copy in near:
         copy.start()
-    pair = [remote(hubs.at[core, mine], hubs.at[core, mine], c_send.at[0], c_recv.at[0], me, other)]
-    pair[0].start()
+    for da, at in ((1, 1), (3, 2), (2, 0)):
+        gather[at].wait_recv()
+        onward[da] = send_on(da)
     twin = []
     for i in range(2):
         near[i].wait_recv()
@@ -181,21 +218,22 @@
         side, at = n // 2, n % 2
         rows = jnp.concatenate([halo[0, side, at].reshape(B, 256), halo[1, side, at].reshape(B, 256)], axis=1)
         i = side * 6 + at
-        node = (first + i - 2 + devices * 4) % (devices * 4)
-        project(rows, w_qkv[1], wv_t[...], usable_of(node), keys, vals, bias, i)
+        project(rows, w_qkv[1], wv_t[...], usable_of(i), keys, vals, bias, i)
 
     @pl.loop(0, 6)
     def _(n):
         meet(n // 2 + n // 3, (n + 1) // 2 + 4 * (n // 3))
 
-    for k in ORDER:
-        gather[k].wait_recv()
-        part, _ = at_plane(k, -1)
-        pair.append(remote(hubs.at[core, part], hubs.at[core, part], c_send.at[k], c_recv.at[k], me, other))
-        pair[-1].start()
+    for da in (0, 1, 3, 2):
+        for n, db in ((1, 1), (2, 3), (0, 2)):
+            onward[da][n].wait_recv()
+            part = part_of(-da, -db)
+            at = 4 + da * 3 + db - 1
+            pair.append(remote(hubs.at[core, part], hubs.at[core, part], c_send.at[at], c_recv.at[at], me, other))
+            pair[-1].start()
     for copy in pair:
         copy.wait()
-    for copy in list(scatter.values()) + lines + spread + list(gather.values()) + near:
+    for copy in list(scatter.values()) + lines + spread + gather + sum(onward.values(), []) + near:
         copy.wait_send()
 
 
@@ -207,9 +245,15 @@
                    jax.ShapeDtypeStruct((4, HEADS_HERE, B, B), BF16),
                    jax.ShapeDtypeStruct((4, HEADS_HERE, TALL, B), F32),
                    jax.ShapeDtypeStruct((4, HEADS_HERE, 1, B), F32)),
-        in_specs=[SMEM, SMEM, SMEM, VMEM, VMEM, VMEM],
+        in_specs=[HBM] * 6,
         out_specs=(VMEM, VMEM, VMEM, VMEM),
         scratch_shapes=[
+            pltpu.SMEM((8,), jnp.int32),
+            pltpu.SMEM((4, 16), jnp.int32),
+            pltpu.SMEM((4,), jnp.int32),
+            pltpu.VMEM((4, 16, 16, 512), BF16),
+            pltpu.VMEM((3, 512, 256), BF16),
+            pltpu.VMEM((8, 1, B), jnp.int32),
             pltpu.VMEM((2, 2, 2, 16, 16, 256), BF16),
             pltpu.VMEM((16, 4, 16, 256), BF16),
             pltpu.VMEM((8, 16, 256), BF16),
@@ -218,18 +262,25 @@
             pltpu.VMEM((8, B, B), BF16),
             pltpu.VMEM((8, HEADS_HERE, TALL, B), BF16),
             pltpu.VMEM((8, B, 128), F32),
-            dma(()),
-            dma((15,)), dma((15,)), dma((7,)), dma((7,)), dma((7,)), dma((7,)), dma((15,)), dma((15,)),
+            dma((6,)), dma((8,)),
+            dma((15,)), dma((15,)), dma((7,)), dma((7,)), dma((7,)), dma((7,)), dma((3,)), dma((3,)),
+            dma((12,)), dma((12,)),
             dma((16,)), dma((16,)), dma((2,)), dma((2,)), dma((2,)), dma((2,)),
         ],
         compiler_params=pltpu.CompilerParams(collective_id=0, has_side_effects=True,
                                              vmem_limit_bytes=40 << 20),
         name="near",
-    )(hub_ids, lists, counts, feat.reshape(4, 16, 16, 512), w_qkv, mask)
+    )(*[pltpu.with_memory_space_constraint(a, pltpu.HBM)
+        for a in (hub_ids, lists, counts, feat.reshape(4, 16, 16, 512), w_qkv, mask)])
 
 
 def hub_kernel(hub_ids, lists, counts, hubs, q_t, acc_in, top_in, w_qkv, mask, out,
-               wv_t, keys, vals, bias, acc, top, att_t, cnt):
+               marks, mark_sem, wv_t, keys, vals, bias, acc, top, att_t, cnt):
+    loads = []
+    for k in range(8):
+        loads.append(pltpu.make_async_copy(mask.at[pl.ds(pl.multiple_of(hub_ids[k] * B, B), B)], marks.at[k, 0],
+                                           mark_sem.at[k]))
+        loads[k].start()
     for b in range(4):
         for i in range(8):
             cnt[b, i] = 0
@@ -238,12 +289,14 @@
     acc[...] = acc_in[...]
     top[...] = top_in[...]
     wv_t[...] = w_qkv[2].T
+    for copy in loads:
+        copy.wait()
 
     @pl.loop(0, 8)
     def _(k):
         rows = jnp.concatenate([
             jnp.concatenate([hubs[c, p, k] for p in range(16)], axis=0) for c in range(2)], axis=1)
-        usable = (mask[pl.ds(hub_ids[k], 1), :] > 0).astype(F32)
+        usable = (marks[k] > 0).astype(F32)
         project(rows, w_qkv[1], wv_t[...], usable, keys, vals, bias, k)
 
     @pl.loop(0, 4)
@@ -265,9 +318,11 @@
     return pl.pallas_call(
         hub_kernel,
         out_shape=jax.ShapeDtypeStruct((1024, 256), BF16),
-        in_specs=[SMEM, SMEM, SMEM] + [VMEM] * 6,
+        in_specs=[SMEM, SMEM, SMEM] + [VMEM] * 5 + [HBM],
         out_specs=VMEM,
         scratch_shapes=[
+            pltpu.VMEM((8, 1, B), jnp.int32),
+            pltpu.SemaphoreType.DMA((8,)),
             pltpu.VMEM((256, 512), BF16),
             pltpu.VMEM((8, B, B), BF16),
             pltpu.VMEM((8, HEADS_HERE, TALL, B), BF16),
@@ -287,7 +342,7 @@
     me = lax.axis_index("head")
     swap = [(0, 1), (1, 0)]
     share = width // 2
-    mask = node_mask.reshape(-1, B)
+    mask = node_mask
     w_mine = lax.dynamic_slice_in_dim(w_out, me * share, share, 1)
     w_sent = lax.dynamic_slice_in_dim(w_out, (1 - me) * share, share, 1)
     w_got = lax.ppermute(w_sent, "head", swap)

time: 73.9 us -> 66 us (0.89)
  local copies, waits for them, and re-layouts: 5.65 us -> 0.04 us
  Pallas kernels: 64.7 us -> 62.5 us
    unnamed x16 -> x14, local copies, waits for them, and re-layouts: 4.36 us -> 0.03 us
    pallas_call x1, Pallas kernels: 12.1 us -> 10.5 us  [hub_attention(): pl.pallas_call(hub_kernel, out_shape=jax.ShapeDtypeStruct((1024, 256), BF...]
    reshape x1 -> x0, local copies, waits for them, and re-layouts: 1.29 us -> none  [body(): mask = node_mask.reshape(-1, B)]
where the time goes in v3:
time: 66 us; the launch traced here: 65.9 us
  Pallas kernels  62.5 us (95%)
  matrix products  1.39 us (2%)
  waiting for transfers between devices  1.19 us (2%)
  starting transfers between devices  0.68 us (1%)
    pallas_call x1, Pallas kernels, near_attention(): pl.pallas_call(near_kernel, out_shape=(jax.ShapeDtypeStruct((2, 16, 8, 16...  52 us
    pallas_call x1, Pallas kernels, hub_attention(): pl.pallas_call(hub_kernel, out_shape=jax.ShapeDtypeStruct((1024, 256), BF...  10.5 us
  transfers between devices with their start and end apart: 2, of which 1 were waited for; matrix products, arithmetic and copies ran while one was open for 0% of the time, Pallas kernels for 0%

profile of v3, /device:TPU:1, one launch (start us, length us, event | category | flops | bytes accessed | tf_op | source)
XLA Modules:
  0.0 65.9 jit_solution(17812590864614762881)
XLA Ops:
  0.0 0.0 copy-start
  0.0 0.0 copy-start.3
  0.0 0.0 copy-start.5
  0.0 0.0 copy-start.2
  0.0 0.0 copy-start.4
  0.0 0.0 copy-start.1
  0.0 52.0 %near.1 = (bf16[2,16,8,16,256]{4,3,2,1,0:T(8,128)(2,1)S(1)}, bf16[4,4,256,256]{3,2,1,0:T(8,128)(2,1)S(1)}, f32[4,4,80,256]{3,2,1,0:T(8,128)S(1)}, f32[4,4,1,256]{3,2,1,0:T(1,128)S(1)}) custom-call(s32[8]{0:T(128)} %hub_ids.1, s32[4,16]{1,0:T(4,128)} %lists.1, s32[4]{0:T(128)} %counts.1, bf16[4,16,16,512]{3,2,1,0:T(8,128)(2,1)} %bitcast.4, ...), custom_call_target="tpu_custom_call" | custom-call | tf_op jit(solution)/shard_map/near/pallas_call | solution.py:242
  52.1 0.0 copy-done.3
  52.1 0.0 copy-done.5
  52.1 0.0 copy-done.2
  52.1 0.0 copy-done.4
  52.1 0.0 copy-done.1
  52.1 10.5 %hub.1 = bf16[1024,256]{1,0:T(8,128)(2,1)S(1)} custom-call(s32[8]{0:T(128)S(1)} %copy-done.4, s32[4,16]{1,0:T(4,128)S(1)} %copy-done.3, s32[4]{0:T(128)S(1)} %copy-done.5, bf16[2,16,8,16,256]{4,3,2,1,0:T(8,128)(2,1)S(1)} %get-tuple-element.9.hubs, bf16[4,4,256,256]{3,2,1,0:T(8,128)(2,1)S(1)} %get-tuple-element.10.q_t, ...), custom_call_target="tpu_custom_call" | custom-call | tf_op jit(solution)/shard_map/hub/pallas_call | solution.py:318
  62.6 0.0 copy-start.6
  62.6 0.5 collective-permute-start
  63.1 0.0 copy-done
  63.1 0.2 collective-permute-start.1
  63.3 0.3 fusion.2
  63.6 1.2 %collective-permute-done.1 = bf16[256,256]{1,0:T(8,128)(2,1)S(1)} collective-permute-done((bf16[256,256]{1,0:T(8,128)(2,1)S(1)}, bf16[256,256]{1,0:T(8,128)(2,1)S(1)}, u32[]{:S(2)}, u32[]{:S(2)}) %collective-permute-start.1) | collective-permute-done | bytes 131104 | tf_op jit(solution)/shard_map/ppermute | solution.py:348
  64.8 0.0 collective-permute-done
  64.8 0.0 copy-done.6
  64.8 1.1 %fusion.1 = bf16[1024,256]{1,0:T(8,128)(2,1)} fusion(f32[1024,256]{1,0:T(8,128)S(1)} %fusion.2, bf16[1024,256]{1,0:T(8,128)(2,1)S(1)} %collective-permute-done, bf16[256,256]{1,0:T(8,128)(2,1)S(1)} %collective-permute-done.1, bf16[1024,512]{1,0:T(8,128)(2,1)S(1)} %copy-done.6, s32[]{:T(128)S(6)} %select_n.7), kind=kOutput, calls=%fused_computation.2 | convolution fusion | flops 135266304 | bytes 2752516 | tf_op jit(solution)/shard_map/dot_general | solution.py:354
  (1 shorter events, 0.0 us)
Async XLA Ops:
  0.0 63.1 %copy-start = (bf16[256,512]{1,0:T(8,128)(2,1)S(1)}, bf16[256,512]{1,0:T(8,128)(2,1)}, u32[]{:S(2)}) copy-start(bf16[256,512]{1,0:T(8,128)(2,1)} %param.9) | copy-start | bytes 786436
  0.0 52.1 %copy-start.3 = (s32[4,16]{1,0:T(4,128)S(1)}, s32[4,16]{1,0:T(4,128)}, u32[]{:S(2)}) copy-start(s32[4,16]{1,0:T(4,128)} %lists.1) | copy-start | bytes 772
  0.0 52.1 %copy-start.5 = (s32[4]{0:T(128)S(1)}, s32[4]{0:T(128)}, u32[]{:S(2)}) copy-start(s32[4]{0:T(128)} %counts.1) | copy-start | bytes 52
  0.0 52.1 %copy-start.2 = (s32[131072]{0:T(1024)S(1)}, s32[131072]{0:T(1024)}, u32[]{:S(2)}) copy-start(s32[131072]{0:T(1024)} %mask.3) | copy-start | bytes 1572868
  0.0 52.1 %copy-start.4 = (s32[8]{0:T(128)S(1)}, s32[8]{0:T(128)}, u32[]{:S(2)}) copy-start(s32[8]{0:T(128)} %hub_ids.1) | copy-start | bytes 100
  0.0 52.1 %copy-start.1 = (bf16[3,512,256]{2,1,0:T(8,128)(2,1)S(1)}, bf16[3,512,256]{2,1,0:T(8,128)(2,1)}, u32[]{:S(2)}) copy-start(bf16[3,512,256]{2,1,0:T(8,128)(2,1)} %w_qkv.1) | copy-start | bytes 2359300
  62.6 2.2 %copy-start.6 = (bf16[1024,512]{1,0:T(8,128)(2,1)S(1)}, bf16[1024,512]{1,0:T(8,128)(2,1)}, u32[]{:S(2)}) copy-start(bf16[1024,512]{1,0:T(8,128)(2,1)} %param.7) | copy-start | bytes 3145732
  62.6 2.2 %collective-permute-start = (bf16[1024,256]{1,0:T(8,128)(2,1)S(1)}, bf16[1024,256]{1,0:T(8,128)(2,1)S(1)}, u32[]{:S(2)}, u32[]{:S(2)}) collective-permute-start(bf16[1024,256]{1,0:T(8,128)(2,1)S(1)} %hub.1), channel_id=1, source_target_pairs={{0,1},{1,0},{2,3},{3,2},{4,5},{5,4},{6,7},{7,6},{8,9},{9,8},{10,11... | collective-permute-start | bytes 1572872 | tf_op jit(solution)/shard_map/ppermute | solution.py:351
  63.1 1.7 %collective-permute-start.1 = (bf16[256,256]{1,0:T(8,128)(2,1)S(1)}, bf16[256,256]{1,0:T(8,128)(2,1)S(1)}, u32[]{:S(2)}, u32[]{:S(2)}) collective-permute-start(bf16[256,256]{1,0:T(8,128)(2,1)S(1)} %constant_dynamic-slice_fusion), channel_id=1, source_target_pairs={{0,1},{1,0},{2,3},{3,2},{4,5},{5,4},{6,7},{7,6},{8,9},{9,8},{10,11... | collective-permute-start | bytes 393224 | tf_op jit(solution)/shard_map/ppermute | solution.py:348

commit v4 on v3

--- a/solution.py
+++ b/solution.py
@@ -28,6 +28,13 @@
         vals[i, h, 0:DH, :] = v_t[h * DH:(h + 1) * DH, :] * usable.astype(BF16)
         vals[i, h, DH:TALL, :] = tail
     bias[i] = jnp.broadcast_to((usable - 1.0) * 1e30, (128, B)).T
+
+
+def squares(rows):
+    r = lax.broadcasted_iota(jnp.int32, (B, 128), 0) // DH
+    pick = (r == lax.broadcasted_iota(jnp.int32, (B, 128), 1)).astype(BF16)
+    rows = rows.astype(F32)
+    return jnp.max(jnp.dot((rows * rows).astype(BF16), pick, preferred_element_type=F32), axis=0, keepdims=True)
 
 
 def attend(q_t, b, kb, vb, low, times, acc, top):
@@ -46,11 +53,11 @@
         top[b, h] = news[h]
 
 
-def near_kernel(hub_ids_at, lists_at, counts_at, feat_at, w_at, mask, hubs, q_t, acc, top,
+def near_kernel(hub_ids_at, lists_at, counts_at, feat_at, w_at, mask, w_out, hubs, q_t, acc, top, norm, w_got,
                 hub_ids, lists, counts, feat, w_qkv, marks,
                 halo, plane, zsend, zrecv, wv_t, keys, vals, bias, local, mark_sem,
                 p_send, p_recv, z_send, z_recv, g_send, g_recv, a_send, a_recv, b_send, b_recv,
-                c_send, c_recv, n_send, n_recv, m_send, m_recv):
+                c_send, c_recv, n_send, n_recv, m_send, m_recv, w_send, w_recv):
     me = lax.axis_index("blk")
     core = lax.axis_index("head")
     devices = lax.axis_size("blk")
@@ -106,6 +113,7 @@
     row_head = lax.broadcasted_iota(jnp.int32, (B, B), 0) // DH
     acc[...] = jnp.zeros_like(acc)
     top[...] = jnp.full_like(top, NEG)
+    norm[...] = jnp.zeros_like(norm)
 
     def usable_of(i):
         return (marks[i] > 0).astype(F32)
@@ -114,6 +122,7 @@
     def _(b):
         rows = feat[b].reshape(B, 512)
         q = jnp.dot(rows, w_qkv[0], preferred_element_type=F32).astype(BF16)
+        norm[...] = jnp.maximum(norm[...], squares(q))
         q = (q * jnp.asarray(DH ** -0.5, BF16)).T
         for h in range(HEADS_HERE):
             q_t[b, h] = jnp.where(row_head == h, q, jnp.zeros_like(q))
@@ -134,6 +143,15 @@
         scatter[k] = remote(feat_at.at[:, part, :, columns], plane.at[mine],
                             p_send.at[k - 1], p_recv.at[k - 1], blk, core)
         scatter[k].start()
+    near = [
+        remote(feat_at.at[2:4, :, :, columns], halo.at[core, 0], n_send.at[0], n_recv.at[0], after, core),
+        remote(feat_at.at[0:2, :, :, columns], halo.at[core, 1], n_send.at[1], n_recv.at[1], before, core),
+    ]
+    for copy in near:
+        copy.start()
+    weights = remote(w_out.at[:, pl.ds(pl.multiple_of(other * 256, 256), 256)], w_got, w_send.at[0], w_recv.at[0],
+                     me, other)
+    weights.start()
 
     @pl.loop(0, 10)
     def _(n):
@@ -166,6 +184,11 @@
         spread.append(remote(hubs.at[core, mine, z], hubs.at[core, mine, z],
                              g_send.at[k - 1], g_recv.at[k - 1], blk, core))
         spread[-1].start()
+    twin = []
+    for i in range(2):
+        near[i].wait_recv()
+        twin.append(remote(halo.at[core, i], halo.at[core, i], m_send.at[i], m_recv.at[i], me, other))
+        twin[i].start()
     for copy in spread:
         copy.wait_recv()
 
@@ -196,22 +219,11 @@
                              me + ((along + da) % 4 - along) * along_blk, core))
         gather[-1].start()
     onward = {0: send_on(0)}
-    near = [
-        remote(feat_at.at[2:4, :, :, columns], halo.at[core, 0], n_send.at[0], n_recv.at[0], after, core),
-        remote(feat_at.at[0:2, :, :, columns], halo.at[core, 1], n_send.at[1], n_recv.at[1], before, core),
-    ]
-    for copy in near:
-        copy.start()
     for da, at in ((1, 1), (3, 2), (2, 0)):
         gather[at].wait_recv()
         onward[da] = send_on(da)
-    twin = []
-    for i in range(2):
-        near[i].wait_recv()
-        twin.append(remote(halo.at[core, i], halo.at[core, i], m_send.at[i], m_recv.at[i], me, other))
-        twin[i].start()
-    for i in range(2):
-        twin[i].wait()
+    for copy in twin:
+        copy.wait()
 
     @pl.loop(0, 4)
     def _(n):
@@ -231,22 +243,24 @@
             at = 4 + da * 3 + db - 1
             pair.append(remote(hubs.at[core, part], hubs.at[core, part], c_send.at[at], c_recv.at[at], me, other))
             pair[-1].start()
-    for copy in pair:
+    for copy in pair + [weights]:
         copy.wait()
     for copy in list(scatter.values()) + lines + spread + gather + sum(onward.values(), []) + near:
         copy.wait_send()
 
 
-def near_attention(hub_ids, lists, counts, feat, w_qkv, mask):
+def near_attention(hub_ids, lists, counts, feat, w_qkv, mask, w_out):
     dma = pltpu.SemaphoreType.DMA
     return pl.pallas_call(
         near_kernel,
         out_shape=(jax.ShapeDtypeStruct((2, 16, 8, 16, 256), BF16),
                    jax.ShapeDtypeStruct((4, HEADS_HERE, B, B), BF16),
                    jax.ShapeDtypeStruct((4, HEADS_HERE, TALL, B), F32),
-                   jax.ShapeDtypeStruct((4, HEADS_HERE, 1, B), F32)),
-        in_specs=[HBM] * 6,
-        out_specs=(VMEM, VMEM, VMEM, VMEM),
+                   jax.ShapeDtypeStruct((4, HEADS_HERE, 1, B), F32),
+                   jax.ShapeDtypeStruct((1, 128), F32),
+                   jax.ShapeDtypeStruct((256, 256), BF16)),
+        in_specs=[HBM] * 7,
+        out_specs=(VMEM,) * 6,
         scratch_shapes=[
             pltpu.SMEM((8,), jnp.int32),
             pltpu.SMEM((4, 16), jnp.int32),
@@ -265,17 +279,17 @@
             dma((6,)), dma((8,)),
             dma((15,)), dma((15,)), dma((7,)), dma((7,)), dma((7,)), dma((7,)), dma((3,)), dma((3,)),
             dma((12,)), dma((12,)),
-            dma((16,)), dma((16,)), dma((2,)), dma((2,)), dma((2,)), dma((2,)),
+            dma((16,)), dma((16,)), dma((2,)), dma((2,)), dma((2,)), dma((2,)), dma((1,)), dma((1,)),
         ],
         compiler_params=pltpu.CompilerParams(collective_id=0, has_side_effects=True,
                                              vmem_limit_bytes=40 << 20),
         name="near",
     )(*[pltpu.with_memory_space_constraint(a, pltpu.HBM)
-        for a in (hub_ids, lists, counts, feat.reshape(4, 16, 16, 512), w_qkv, mask)])
-
-
-def hub_kernel(hub_ids, lists, counts, hubs, q_t, acc_in, top_in, w_qkv, mask, out,
-               marks, mark_sem, wv_t, keys, vals, bias, acc, top, att_t, cnt):
+        for a in (hub_ids, lists, counts, feat.reshape(4, 16, 16, 512), w_qkv, mask, w_out)])
+
+
+def hub_kernel(hub_ids, lists, counts, hubs, q_t, acc_in, top_in, norm, w_qkv, mask, out, acc, top,
+               marks, mark_sem, wv_t, keys, vals, bias, att_t, cnt):
     loads = []
     for k in range(8):
         loads.append(pltpu.make_async_copy(mask.at[pl.ds(pl.multiple_of(hub_ids[k] * B, B), B)], marks.at[k, 0],
@@ -286,40 +300,66 @@
             cnt[b, i] = 0
         for j in range(1, 5):
             cnt[b, lists[b, j]] += jnp.where(j < counts[b], 1, 0)
-    acc[...] = acc_in[...]
-    top[...] = top_in[...]
     wv_t[...] = w_qkv[2].T
     for copy in loads:
         copy.wait()
 
-    @pl.loop(0, 8)
-    def _(k):
+    def prepare(k, longest):
         rows = jnp.concatenate([
             jnp.concatenate([hubs[c, p, k] for p in range(16)], axis=0) for c in range(2)], axis=1)
         usable = (marks[k] > 0).astype(F32)
         project(rows, w_qkv[1], wv_t[...], usable, keys, vals, bias, k)
+        return jnp.maximum(longest, squares(keys[k]))
+
+    longest = lax.fori_loop(0, 8, prepare, jnp.zeros((1, 128), F32))
+    reach = jnp.sqrt(jnp.max(longest * norm[...]) * 1.02) * DH ** -0.5 + jnp.max(jnp.abs(top[...]))
+    close = reach <= 40.0
+    heads = range(HEADS_HERE)
+
+    def over_hubs(step):
+        @pl.loop(0, 4)
+        def _(b):
+            @pl.loop(0, 8)
+            def _(k):
+                times = cnt[b, k]
+
+                @pl.when(times > 0)
+                def _():
+                    step(b, k, times)
+
+    @pl.when(close)
+    def _():
+        def step(b, k, times):
+            kb = keys[k]
+            scale = times.astype(F32)
+            ss = [jnp.dot(kb, q_t[b, h], preferred_element_type=F32) for h in heads]
+            ps = [jnp.exp(ss[h] - top[b, h]).astype(BF16) for h in heads]
+            got = [jnp.dot(vals[k, h], ps[h], preferred_element_type=F32) for h in heads]
+            for h in heads:
+                acc[b, h] += scale * got[h]
+
+        over_hubs(step)
+
+    @pl.when(jnp.logical_not(close))
+    def _():
+        over_hubs(lambda b, k, times: attend(q_t, b, keys[k], vals.at[k], bias[k], times, acc, top))
 
     @pl.loop(0, 4)
     def _(b):
-        @pl.loop(0, 8)
-        def _(k):
-            times = cnt[b, k]
-
-            @pl.when(times > 0)
-            def _():
-                attend(q_t, b, keys[k], vals.at[k], bias[k], times, acc, top)
-
-        for h in range(HEADS_HERE):
-            att_t[h * DH:(h + 1) * DH, :] = (acc[b, h, 0:DH, :] / acc[b, h, DH:DH + 1, :]).astype(BF16)
+        for h in heads:
+            att_t[h * DH:(h + 1) * DH, :] = (acc[b, h, 0:DH, :] * (1.0 / acc[b, h, DH:DH + 1, :])).astype(BF16)
         out[pl.ds(pl.multiple_of(b * B, B), B), :] = att_t[...].T
 
 
-def hub_attention(hub_ids, lists, counts, hubs, q_t, acc, top, w_qkv, mask):
+def hub_attention(hub_ids, lists, counts, hubs, q_t, acc, top, norm, w_qkv, mask):
     return pl.pallas_call(
         hub_kernel,
-        out_shape=jax.ShapeDtypeStruct((1024, 256), BF16),
-        in_specs=[SMEM, SMEM, SMEM] + [VMEM] * 5 + [HBM],
-        out_specs=VMEM,
+        out_shape=(jax.ShapeDtypeStruct((1024, 256), BF16),
+                   jax.ShapeDtypeStruct(acc.shape, F32),
+                   jax.ShapeDtypeStruct(top.shape, F32)),
+        in_specs=[SMEM, SMEM, SMEM] + [VMEM] * 6 + [HBM],
+        out_specs=(VMEM,) * 3,
+        input_output_aliases={5: 1, 6: 2},
         scratch_shapes=[
             pltpu.VMEM((8, 1, B), jnp.int32),
             pltpu.SemaphoreType.DMA((8,)),
@@ -327,28 +367,23 @@
             pltpu.VMEM((8, B, B), BF16),
             pltpu.VMEM((8, HEADS_HERE, TALL, B), BF16),
             pltpu.VMEM((8, B, 128), F32),
-            pltpu.VMEM((4, HEADS_HERE, TALL, B), F32),
-            pltpu.VMEM((4, HEADS_HERE, 1, B), F32),
             pltpu.VMEM((B, B), BF16),
             pltpu.SMEM((4, 8), jnp.int32),
         ],
         compiler_params=pltpu.CompilerParams(vmem_limit_bytes=40 << 20),
         name="hub",
-    )(hub_ids, lists, counts, hubs, q_t, acc, top, w_qkv, mask)
+    )(hub_ids, lists, counts, hubs, q_t, acc, top, norm, w_qkv, mask)[0]
 
 
 def body(features, w_qkv, w_out, key_lists, key_counts, node_mask, hub_ids):
     width = features.shape[1]
     me = lax.axis_index("head")
-    swap = [(0, 1), (1, 0)]
     share = width // 2
     mask = node_mask
     w_mine = lax.dynamic_slice_in_dim(w_out, me * share, share, 1)
-    w_sent = lax.dynamic_slice_in_dim(w_out, (1 - me) * share, share, 1)
-    w_got = lax.ppermute(w_sent, "head", swap)
-    hubs, q_t, acc, top = near_attention(hub_ids, key_lists, key_counts, features, w_qkv, mask)
-    attended = hub_attention(hub_ids, key_lists, key_counts, hubs, q_t, acc, top, w_qkv, mask)
-    theirs = lax.ppermute(attended, "head", swap)
+    hubs, q_t, acc, top, norm, w_got = near_attention(hub_ids, key_lists, key_counts, features, w_qkv, mask, w_out)
+    attended = hub_attention(hub_ids, key_lists, key_counts, hubs, q_t, acc, top, norm, w_qkv, mask)
+    theirs = lax.ppermute(attended, "head", [(0, 1), (1, 0)])
     resid = lax.dynamic_slice_in_dim(features, me * share, share, 1)
     mixed = (jnp.dot(attended, w_mine, preferred_element_type=F32)
              + jnp.dot(theirs, w_got, preferred_element_type=F32) + resid.astype(F32))

time: 66 us -> 68.5 us (1.038)
  Pallas kernels: 62.5 us -> 65.2 us
    pallas_call x1, Pallas kernels: 10.5 us -> 14.8 us  [hub_attention(): pl.pallas_call(hub_kernel, out_shape=(jax.ShapeDtypeStruct((1024, 256), B...]
    pallas_call x1, Pallas kernels: 52 us -> 50.4 us  [near_attention(): pl.pallas_call(near_kernel, out_shape=(jax.ShapeDtypeStruct((2, 16, 8, 16...]
    ppermute x2 -> x1, waiting for transfers between devices: 1.19 us -> 1.47 us  [body(): theirs = lax.ppermute(attended, 'head', [(0, 1), (1, 0)])]
  transfers between devices with their start and end apart: 2 -> 1, of which waited for: 1 -> 1; matrix products, arithmetic and copies ran while one was open for 0% -> 0% of each run, Pallas kernels for 0% -> 0%
where the time goes in v4:
time: 68.5 us; the launch traced here: 68.4 us
  Pallas kernels  65.2 us (95%)
  waiting for transfers between devices  1.47 us (2%)
  matrix products  1.38 us (2%)
    pallas_call x1, Pallas kernels, near_attention(): pl.pallas_call(near_kernel, out_shape=(jax.ShapeDtypeStruct((2, 16, 8, 16...  50.4 us
    pallas_call x1, Pallas kernels, hub_attention(): pl.pallas_call(hub_kernel, out_shape=(jax.ShapeDtypeStruct((1024, 256), B...  14.8 us
    ppermute x1, waiting for transfers between devices, body(): theirs = lax.ppermute(attended, 'head', [(0, 1), (1, 0)])  1.47 us
  transfers between devices with their start and end apart: 1, of which 1 were waited for; matrix products, arithmetic and copies ran while one was open for 0% of the time, Pallas kernels for 0%

profile of v4, /device:TPU:1, one launch (start us, length us, event | category | flops | bytes accessed | tf_op | source)
XLA Modules:
  0.0 68.4 jit_solution(4955505851442314782)
XLA Ops:
  0.0 0.0 copy-start.2
  0.0 0.0 copy-start.4
  0.0 0.0 copy-start.1
  0.0 0.0 copy-start.3
  0.0 0.0 copy-start
  0.0 50.4 %near.1 = (bf16[2,16,8,16,256]{4,3,2,1,0:T(8,128)(2,1)S(1)}, bf16[4,4,256,256]{3,2,1,0:T(8,128)(2,1)S(1)}, f32[4,4,80,256]{3,2,1,0:T(8,128)S(1)}, f32[4,4,1,256]...) custom-call(s32[8]{0:T(128)} %hub_ids.1, s32[4,16]{1,0:T(4,128)} %lists.1, s32[4]{0:T(128)} %counts.1, ...), custom_call_target="tpu_custom_call" | custom-call | tf_op jit(solution)/shard_map/near/pallas_call | solution.py:254
  50.5 0.0 copy-done.2
  50.5 0.0 copy-done.4
  50.5 0.0 copy-done.1
  50.5 0.0 copy-done.3
  50.5 0.0 copy-done
  50.5 0.0 copy-start.6
  50.5 0.0 copy-start.5
  50.6 14.8 %hub.1 = (bf16[1024,256]{1,0:T(8,128)(2,1)S(1)}, f32[4,4,80,256]{3,2,1,0:T(8,128)S(1)}, f32[4,4,1,256]{3,2,1,0:T(1,128)S(1)}) custom-call(s32[8]{0:T(128)S(1)} %copy-done.3, s32[4,16]{1,0:T(4,128)S(1)} %copy-done.2, s32[4]{0:T(128)S(1)} %copy-done.4, ...), custom_call_target="tpu_custom_call", output_to_operand_aliasing={{1}: (5, {}), {2}: (6, {})} | custom-call | tf_op jit(solution)/shard_map/hub/pallas_call | solution.py:355
  65.3 0.2 collective-permute-start
  65.5 0.0 copy-done.6
  65.5 0.3 fusion.2
  65.8 1.5 %collective-permute-done = bf16[1024,256]{1,0:T(8,128)(2,1)S(1)} collective-permute-done((bf16[1024,256]{1,0:T(8,128)(2,1)S(1)}, bf16[1024,256]{1,0:T(8,128)(2,1)S(1)}, u32[]{:S(2)}, u32[]{:S(2)}) %collective-permute-start) | collective-permute-done | bytes 524320 | tf_op jit(solution)/shard_map/ppermute | solution.py:386
  67.3 0.0 copy-done.5
  67.3 1.1 %fusion.1 = bf16[1024,256]{1,0:T(8,128)(2,1)} fusion(f32[1024,256]{1,0:T(8,128)S(1)} %fusion.2, bf16[1024,256]{1,0:T(8,128)(2,1)S(1)} %collective-permute-done, bf16[256,256]{1,0:T(8,128)(2,1)S(1)} %get-tuple-element.18, bf16[1024,512]{1,0:T(8,128)(2,1)S(1)} %copy-done.5, s32[]{:T(128)S(6)} %select_n.4), kind=kOutput, calls=%fused_computation.2 | convolution fusion | flops 135266304 | bytes 2752516 | tf_op jit(solution)/shard_map/dot_general | solution.py:389
Async XLA Ops:
  0.0 50.5 %copy-start.2 = (s32[4,16]{1,0:T(4,128)S(1)}, s32[4,16]{1,0:T(4,128)}, u32[]{:S(2)}) copy-start(s32[4,16]{1,0:T(4,128)} %lists.1) | copy-start | bytes 772
  0.0 50.5 %copy-start.4 = (s32[4]{0:T(128)S(1)}, s32[4]{0:T(128)}, u32[]{:S(2)}) copy-start(s32[4]{0:T(128)} %counts.1) | copy-start | bytes 52
  0.0 50.5 %copy-start.1 = (s32[131072]{0:T(1024)S(1)}, s32[131072]{0:T(1024)}, u32[]{:S(2)}) copy-start(s32[131072]{0:T(1024)} %mask.3) | copy-start | bytes 1572868
  0.0 50.5 %copy-start.3 = (s32[8]{0:T(128)S(1)}, s32[8]{0:T(128)}, u32[]{:S(2)}) copy-start(s32[8]{0:T(128)} %hub_ids.1) | copy-start | bytes 100
  0.0 50.5 %copy-start = (bf16[3,512,256]{2,1,0:T(8,128)(2,1)S(1)}, bf16[3,512,256]{2,1,0:T(8,128)(2,1)}, u32[]{:S(2)}) copy-start(bf16[3,512,256]{2,1,0:T(8,128)(2,1)} %w_qkv.1) | copy-start | bytes 2359300
  50.5 15.0 %copy-start.6 = (bf16[256,512]{1,0:T(8,128)(2,1)S(1)}, bf16[256,512]{1,0:T(8,128)(2,1)}, u32[]{:S(2)}) copy-start(bf16[256,512]{1,0:T(8,128)(2,1)} %w_out.1) | copy-start | bytes 786436
  50.5 16.8 %copy-start.5 = (bf16[1024,512]{1,0:T(8,128)(2,1)S(1)}, bf16[1024,512]{1,0:T(8,128)(2,1)}, u32[]{:S(2)}) copy-start(bf16[1024,512]{1,0:T(8,128)(2,1)} %param.7) | copy-start | bytes 3145732
  65.3 2.0 %collective-permute-start = (bf16[1024,256]{1,0:T(8,128)(2,1)S(1)}, bf16[1024,256]{1,0:T(8,128)(2,1)S(1)}, u32[]{:S(2)}, u32[]{:S(2)}) collective-permute-start(bf16[1024,256]{1,0:T(8,128)(2,1)S(1)} %get-tuple-element.17), channel_id=1, source_target_pairs={{0,1},{1,0},{2,3},{3,2},{4,5},{5,4},{6,7},{7,6},{8,9},{9,8},{10,11... | collective-permute-start | bytes 1572872 | tf_op jit(solution)/shard_map/ppermute | solution.py:386

commit v5 on v4

--- a/solution.py
+++ b/solution.py
@@ -13,6 +13,7 @@
 TALL = DH + 16
 NT = (((1,), (1,)), ((), ()))
 NEG = -1e30
+EARLY = 6
 MESH = pl.DeviceIdType.MESH
 VMEM = pl.BlockSpec(memory_space=pltpu.VMEM)
 SMEM = pl.BlockSpec(memory_space=pltpu.SMEM)
@@ -53,9 +54,10 @@
         top[b, h] = news[h]
 
 
-def near_kernel(hub_ids_at, lists_at, counts_at, feat_at, w_at, mask, w_out, hubs, q_t, acc, top, norm, w_got,
+def near_kernel(hub_ids_at, lists_at, counts_at, feat_at, w_at, mask, w_out,
+                hubs, q_t, acc, top, norm, w_got, wk, wv_t,
                 hub_ids, lists, counts, feat, w_qkv, marks,
-                halo, plane, zsend, zrecv, wv_t, keys, vals, bias, local, mark_sem,
+                halo, plane, zsend, zrecv, keys, vals, bias, local, mark_sem,
                 p_send, p_recv, z_send, z_recv, g_send, g_recv, a_send, a_recv, b_send, b_recv,
                 c_send, c_recv, n_send, n_recv, m_send, m_recv, w_send, w_recv):
     me = lax.axis_index("blk")
@@ -106,35 +108,6 @@
                                            mark_sem.at[i]))
     for copy in loads:
         copy.start()
-    for copy in loads:
-        copy.wait()
-
-    wv_t[...] = w_qkv[2].T
-    row_head = lax.broadcasted_iota(jnp.int32, (B, B), 0) // DH
-    acc[...] = jnp.zeros_like(acc)
-    top[...] = jnp.full_like(top, NEG)
-    norm[...] = jnp.zeros_like(norm)
-
-    def usable_of(i):
-        return (marks[i] > 0).astype(F32)
-
-    @pl.loop(0, 4)
-    def _(b):
-        rows = feat[b].reshape(B, 512)
-        q = jnp.dot(rows, w_qkv[0], preferred_element_type=F32).astype(BF16)
-        norm[...] = jnp.maximum(norm[...], squares(q))
-        q = (q * jnp.asarray(DH ** -0.5, BF16)).T
-        for h in range(HEADS_HERE):
-            q_t[b, h] = jnp.where(row_head == h, q, jnp.zeros_like(q))
-        project(rows, w_qkv[1], wv_t[...], usable_of(b + 2), keys, vals, bias, b + 2)
-
-    def meet(b, i):
-        times = jnp.int32(0)
-        for j in [0] + list(range(5, 16)):
-            hit = (lists[b, j] == first + i - 2) & (j < counts[b])
-            times = times + jnp.where(hit, 1, 0)
-        attend(q_t, b, keys[i], vals.at[i], bias[i], times, acc, top)
-
     pl.semaphore_wait(barrier, 25)
 
     scatter = {}
@@ -153,10 +126,40 @@
                      me, other)
     weights.start()
 
-    @pl.loop(0, 10)
-    def _(n):
+    for copy in loads:
+        copy.wait()
+    wk[...] = w_qkv[1]
+    wv_t[...] = w_qkv[2].T
+    row_head = lax.broadcasted_iota(jnp.int32, (B, B), 0) // DH
+    acc[...] = jnp.zeros_like(acc)
+    top[...] = jnp.full_like(top, NEG)
+    norm[...] = jnp.zeros_like(norm)
+
+    def usable_of(i):
+        return (marks[i] > 0).astype(F32)
+
+    @pl.loop(0, 4)
+    def _(b):
+        rows = feat[b].reshape(B, 512)
+        q = jnp.dot(rows, w_qkv[0], preferred_element_type=F32).astype(BF16)
+        norm[...] = jnp.maximum(norm[...], squares(q))
+        q = (q * jnp.asarray(DH ** -0.5, BF16)).T
+        for h in range(HEADS_HERE):
+            q_t[b, h] = jnp.where(row_head == h, q, jnp.zeros_like(q))
+        project(rows, w_qkv[1], wv_t[...], usable_of(b + 2), keys, vals, bias, b + 2)
+
+    def meet(b, i):
+        times = jnp.int32(0)
+        for j in [0] + list(range(5, 16)):
+            hit = (lists[b, j] == first + i - 2) & (j < counts[b])
+            times = times + jnp.where(hit, 1, 0)
+        attend(q_t, b, keys[i], vals.at[i], bias[i], times, acc, top)
+
+    def close_pair(n):
         b = (n + 1) // 3
         meet(b, b + 1 + (n + 1) % 3)
+
+    pl.loop(0, EARLY)(close_pair)
 
     for copy in scatter.values():
         copy.wait_recv()
@@ -170,11 +173,7 @@
         lines[-1].start()
     zrecv[z] = zsend[z]
 
-    @pl.loop(0, 4)
-    def _(n):
-        b = (n % 2) * 2 + n // 2
-        meet(b, (b + 2) % 4 + 2)
-
+    pl.loop(EARLY, 10)(close_pair)
     for copy in lines:
         copy.wait_recv()
     hubs[core, mine, z] = zrecv[lax.rem(lax.div(hub_ids[z], 4), 8)]
@@ -184,6 +183,11 @@
         spread.append(remote(hubs.at[core, mine, z], hubs.at[core, mine, z],
                              g_send.at[k - 1], g_recv.at[k - 1], blk, core))
         spread[-1].start()
+    @pl.loop(0, 4)
+    def _(n):
+        b = (n % 2) * 2 + n // 2
+        meet(b, (b + 2) % 4 + 2)
+
     twin = []
     for i in range(2):
         near[i].wait_recv()
@@ -258,9 +262,11 @@
                    jax.ShapeDtypeStruct((4, HEADS_HERE, TALL, B), F32),
                    jax.ShapeDtypeStruct((4, HEADS_HERE, 1, B), F32),
                    jax.ShapeDtypeStruct((1, 128), F32),
-                   jax.ShapeDtypeStruct((256, 256), BF16)),
+                   jax.ShapeDtypeStruct((256, 256), BF16),
+                   jax.ShapeDtypeStruct((512, 256), BF16),
+                   jax.ShapeDtypeStruct((256, 512), BF16)),
         in_specs=[HBM] * 7,
-        out_specs=(VMEM,) * 6,
+        out_specs=(VMEM,) * 8,
         scratch_shapes=[
             pltpu.SMEM((8,), jnp.int32),
             pltpu.SMEM((4, 16), jnp.int32),
@@ -272,7 +278,6 @@
             pltpu.VMEM((16, 4, 16, 256), BF16),
             pltpu.VMEM((8, 16, 256), BF16),
             pltpu.VMEM((8, 16, 256), BF16),
-            pltpu.VMEM((256, 512), BF16),
             pltpu.VMEM((8, B, B), BF16),
             pltpu.VMEM((8, HEADS_HERE, TALL, B), BF16),
             pltpu.VMEM((8, B, 128), F32),
@@ -288,8 +293,8 @@
         for a in (hub_ids, lists, counts, feat.reshape(4, 16, 16, 512), w_qkv, mask, w_out)])
 
 
-def hub_kernel(hub_ids, lists, counts, hubs, q_t, acc_in, top_in, norm, w_qkv, mask, out, acc, top,
-               marks, mark_sem, wv_t, keys, vals, bias, att_t, cnt):
+def hub_kernel(hub_ids, lists, counts, hubs, q_t, acc_in, top_in, norm, wk, wv_t, mask, out, acc, top,
+               marks, mark_sem, keys, vals, bias, att_t, cnt):
     loads = []
     for k in range(8):
         loads.append(pltpu.make_async_copy(mask.at[pl.ds(pl.multiple_of(hub_ids[k] * B, B), B)], marks.at[k, 0],
@@ -300,18 +305,14 @@
             cnt[b, i] = 0
         for j in range(1, 5):
             cnt[b, lists[b, j]] += jnp.where(j < counts[b], 1, 0)
-    wv_t[...] = w_qkv[2].T
-    for copy in loads:
-        copy.wait()
-
-    def prepare(k, longest):
+    longest = jnp.zeros((1, 128), F32)
+    for k in range(8):
         rows = jnp.concatenate([
             jnp.concatenate([hubs[c, p, k] for p in range(16)], axis=0) for c in range(2)], axis=1)
+        loads[k].wait()
         usable = (marks[k] > 0).astype(F32)
-        project(rows, w_qkv[1], wv_t[...], usable, keys, vals, bias, k)
-        return jnp.maximum(longest, squares(keys[k]))
-
-    longest = lax.fori_loop(0, 8, prepare, jnp.zeros((1, 128), F32))
+        project(rows, wk[...], wv_t[...], usable, keys, vals, bias, k)
+        longest = jnp.maximum(longest, squares(keys[k]))
     reach = jnp.sqrt(jnp.max(longest * norm[...]) * 1.02) * DH ** -0.5 + jnp.max(jnp.abs(top[...]))
     close = reach <= 40.0
     heads = range(HEADS_HERE)
@@ -351,19 +352,18 @@
         out[pl.ds(pl.multiple_of(b * B, B), B), :] = att_t[...].T
 
 
-def hub_attention(hub_ids, lists, counts, hubs, q_t, acc, top, norm, w_qkv, mask):
+def hub_attention(hub_ids, lists, counts, hubs, q_t, acc, top, norm, wk, wv_t, mask):
     return pl.pallas_call(
         hub_kernel,
         out_shape=(jax.ShapeDtypeStruct((1024, 256), BF16),
                    jax.ShapeDtypeStruct(acc.shape, F32),
                    jax.ShapeDtypeStruct(top.shape, F32)),
-        in_specs=[SMEM, SMEM, SMEM] + [VMEM] * 6 + [HBM],
+        in_specs=[SMEM, SMEM, SMEM] + [VMEM] * 7 + [HBM],
         out_specs=(VMEM,) * 3,
         input_output_aliases={5: 1, 6: 2},
         scratch_shapes=[
             pltpu.VMEM((8, 1, B), jnp.int32),
             pltpu.SemaphoreType.DMA((8,)),
-            pltpu.VMEM((256, 512), BF16),
             pltpu.VMEM((8, B, B), BF16),
             pltpu.VMEM((8, HEADS_HERE, TALL, B), BF16),
             pltpu.VMEM((8, B, 128), F32),
@@ -372,7 +372,7 @@
         ],
         compiler_params=pltpu.CompilerParams(vmem_limit_bytes=40 << 20),
         name="hub",
-    )(hub_ids, lists, counts, hubs, q_t, acc, top, norm, w_qkv, mask)[0]
+    )(hub_ids, lists, counts, hubs, q_t, acc, top, norm, wk, wv_t, mask)[0]
 
 
 def body(features, w_qkv, w_out, key_lists, key_counts, node_mask, hub_ids):
@@ -381,8 +381,9 @@
     share = width // 2
     mask = node_mask
     w_mine = lax.dynamic_slice_in_dim(w_out, me * share, share, 1)
-    hubs, q_t, acc, top, norm, w_got = near_attention(hub_ids, key_lists, key_counts, features, w_qkv, mask, w_out)
-    attended = hub_attention(hub_ids, key_lists, key_counts, hubs, q_t, acc, top, norm, w_qkv, mask)
+    hubs, q_t, acc, top, norm, w_got, wk, wv_t = near_attention(
+        hub_ids, key_lists, key_counts, features, w_qkv, mask, w_out)
+    attended = hub_attention(hub_ids, key_lists, key_counts, hubs, q_t, acc, top, norm, wk, wv_t, mask)
     theirs = lax.ppermute(attended, "head", [(0, 1), (1, 0)])
     resid = lax.dynamic_slice_in_dim(features, me * share, share, 1)
     mixed = (jnp.dot(attended, w_mine, preferred_element_type=F32)

time: 68.5 us -> 67.2 us (0.981)
  the two profiles are of different devices: /device:TPU:1 before, /device:TPU:3 now
where the time goes in v5:
time: 67.2 us; the launch traced here: 67.1 us
  Pallas kernels  63.9 us (95%)
  waiting for transfers between devices  1.47 us (2%)
  matrix products  1.39 us (2%)
    pallas_call x1, Pallas kernels, near_attention(): pl.pallas_call(near_kernel, out_shape=(jax.ShapeDtypeStruct((2, 16, 8, 16...  49.6 us
    pallas_call x1, Pallas kernels, hub_attention(): pl.pallas_call(hub_kernel, out_shape=(jax.ShapeDtypeStruct((1024, 256), B...  14.3 us
    ppermute x1, waiting for transfers between devices, body(): theirs = lax.ppermute(attended, 'head', [(0, 1), (1, 0)])  1.47 us
  transfers between devices with their start and end apart: 1, of which 1 were waited for; matrix products, arithmetic and copies ran while one was open for 0% of the time, Pallas kernels for 0%

profile of v5, /device:TPU:3, one launch (start us, length us, event | category | flops | bytes accessed | tf_op | source)
XLA Modules:
  0.0 67.1 jit_solution(12068772179084483399)
XLA Ops:
  0.0 0.0 copy-start.1
  0.0 0.0 copy-start.3
  0.0 0.0 copy-start
  0.0 0.0 copy-start.2
  0.0 49.6 %near.1 = (bf16[2,16,8,16,256]{4,3,2,1,0:T(8,128)(2,1)S(1)}, bf16[4,4,256,256]{3,2,1,0:T(8,128)(2,1)S(1)}, f32[4,4,80,256]{3,2,1,0:T(8,128)S(1)}, f32[4,4,1,256]...) custom-call(s32[8]{0:T(128)} %hub_ids.1, ...), custom_call_target="tpu_custom_call" | custom-call | tf_op jit(solution)/shard_map/near/pallas_call | solution.py:258
  49.7 0.0 copy-done.1
  49.7 0.0 copy-done.3
  49.7 0.0 copy-done
  49.7 0.0 copy-done.2
  49.7 0.0 copy-start.5
  49.7 0.0 copy-start.4
  49.7 14.3 %hub.1 = (bf16[1024,256]{1,0:T(8,128)(2,1)S(1)}, f32[4,4,80,256]{3,2,1,0:T(8,128)S(1)}, f32[4,4,1,256]{3,2,1,0:T(1,128)S(1)}) custom-call(s32[8]{0:T(128)S(1)} %copy-done.2, s32[4,16]{1,0:T(4,128)S(1)} %copy-done.1, s32[4]{0:T(128)S(1)} %copy-done.3, ...), custom_call_target="tpu_custom_call", output_to_operand_aliasing={{1}: (5, {}), {2}: (6, {})} | custom-call | tf_op jit(solution)/shard_map/hub/pallas_call | solution.py:356
  64.0 0.2 collective-permute-start
  64.2 0.0 copy-done.5
  64.2 0.3 fusion.2
  64.5 1.5 %collective-permute-done = bf16[1024,256]{1,0:T(8,128)(2,1)S(1)} collective-permute-done((bf16[1024,256]{1,0:T(8,128)(2,1)S(1)}, bf16[1024,256]{1,0:T(8,128)(2,1)S(1)}, u32[]{:S(2)}, u32[]{:S(2)}) %collective-permute-start) | collective-permute-done | bytes 524320 | tf_op jit(solution)/shard_map/ppermute | solution.py:387
  66.0 0.0 copy-done.4
  66.0 1.1 %fusion.1 = bf16[1024,256]{1,0:T(8,128)(2,1)} fusion(f32[1024,256]{1,0:T(8,128)S(1)} %fusion.2, bf16[1024,256]{1,0:T(8,128)(2,1)S(1)} %collective-permute-done, bf16[256,256]{1,0:T(8,128)(2,1)S(1)} %get-tuple-element.22, bf16[1024,512]{1,0:T(8,128)(2,1)S(1)} %copy-done.4, s32[]{:T(128)S(6)} %select_n.4), kind=kOutput, calls=%fused_computation.2 | convolution fusion | flops 135266304 | bytes 2752516 | tf_op jit(solution)/shard_map/dot_general | solution.py:390
Async XLA Ops:
  0.0 49.7 %copy-start.1 = (s32[4,16]{1,0:T(4,128)S(1)}, s32[4,16]{1,0:T(4,128)}, u32[]{:S(2)}) copy-start(s32[4,16]{1,0:T(4,128)} %lists.1) | copy-start | bytes 772
  0.0 49.7 %copy-start.3 = (s32[4]{0:T(128)S(1)}, s32[4]{0:T(128)}, u32[]{:S(2)}) copy-start(s32[4]{0:T(128)} %counts.1) | copy-start | bytes 52
  0.0 49.7 %copy-start = (s32[131072]{0:T(1024)S(1)}, s32[131072]{0:T(1024)}, u32[]{:S(2)}) copy-start(s32[131072]{0:T(1024)} %mask.3) | copy-start | bytes 1572868
  0.0 49.7 %copy-start.2 = (s32[8]{0:T(128)S(1)}, s32[8]{0:T(128)}, u32[]{:S(2)}) copy-start(s32[8]{0:T(128)} %hub_ids.1) | copy-start | bytes 100
  49.7 14.5 %copy-start.5 = (bf16[256,512]{1,0:T(8,128)(2,1)S(1)}, bf16[256,512]{1,0:T(8,128)(2,1)}, u32[]{:S(2)}) copy-start(bf16[256,512]{1,0:T(8,128)(2,1)} %w_out.1) | copy-start | bytes 786436
  49.7 16.3 %copy-start.4 = (bf16[1024,512]{1,0:T(8,128)(2,1)S(1)}, bf16[1024,512]{1,0:T(8,128)(2,1)}, u32[]{:S(2)}) copy-start(bf16[1024,512]{1,0:T(8,128)(2,1)} %param.7) | copy-start | bytes 3145732
  64.0 2.0 %collective-permute-start = (bf16[1024,256]{1,0:T(8,128)(2,1)S(1)}, bf16[1024,256]{1,0:T(8,128)(2,1)S(1)}, u32[]{:S(2)}, u32[]{:S(2)}) collective-permute-start(bf16[1024,256]{1,0:T(8,128)(2,1)S(1)} %get-tuple-element.21), channel_id=1, source_target_pairs={{0,1},{1,0},{2,3},{3,2},{4,5},{5,4},{6,7},{7,6},{8,9},{9,8},{10,11... | collective-permute-start | bytes 1572872 | tf_op jit(solution)/shard_map/ppermute | solution.py:387

commit v6 on v5

--- a/solution.py
+++ b/solution.py
@@ -120,8 +120,6 @@
         remote(feat_at.at[2:4, :, :, columns], halo.at[core, 0], n_send.at[0], n_recv.at[0], after, core),
         remote(feat_at.at[0:2, :, :, columns], halo.at[core, 1], n_send.at[1], n_recv.at[1], before, core),
     ]
-    for copy in near:
-        copy.start()
     weights = remote(w_out.at[:, pl.ds(pl.multiple_of(other * 256, 256), 256)], w_got, w_send.at[0], w_recv.at[0],
                      me, other)
     weights.start()
@@ -172,6 +170,8 @@
         lines.append(remote(zsend.at[zz], zrecv.at[z], z_send.at[k - 1], z_recv.at[k - 1], blk, core))
         lines[-1].start()
     zrecv[z] = zsend[z]
+    for copy in near:
+        copy.start()
 
     pl.loop(EARLY, 10)(close_pair)
     for copy in lines:

time: 67.2 us -> 61.5 us (0.915)
  Pallas kernels: 63.9 us -> 58.2 us
    pallas_call x1, Pallas kernels: 49.6 us -> 44.6 us  [near_attention(): pl.pallas_call(near_kernel, out_shape=(jax.ShapeDtypeStruct((2, 16, 8, 16...]
where the time goes in v6:
time: 61.5 us; the launch traced here: 61.4 us
  Pallas kernels  58.2 us (95%)
  waiting for transfers between devices  1.44 us (2%)
  matrix products  1.39 us (2%)
    pallas_call x1, Pallas kernels, near_attention(): pl.pallas_call(near_kernel, out_shape=(jax.ShapeDtypeStruct((2, 16, 8, 16...  44.6 us
    pallas_call x1, Pallas kernels, hub_attention(): pl.pallas_call(hub_kernel, out_shape=(jax.ShapeDtypeStruct((1024, 256), B...  13.6 us
    ppermute x1, waiting for transfers between devices, body(): theirs = lax.ppermute(attended, 'head', [(0, 1), (1, 0)])  1.44 us
  transfers between devices with their start and end apart: 1, of which 1 were waited for; matrix products, arithmetic and copies ran while one was open for 0% of the time, Pallas kernels for 0%

profile of v6, /device:TPU:3, one launch (start us, length us, event | category | flops | bytes accessed | tf_op | source)
XLA Modules:
  0.0 61.4 jit_solution(7942706462334575712)
XLA Ops:
  0.0 0.0 copy-start.1
  0.0 0.0 copy-start.3
  0.0 0.0 copy-start
  0.0 0.0 copy-start.2
  0.0 44.6 %near.1 = (bf16[2,16,8,16,256]{4,3,2,1,0:T(8,128)(2,1)S(1)}, bf16[4,4,256,256]{3,2,1,0:T(8,128)(2,1)S(1)}, f32[4,4,80,256]{3,2,1,0:T(8,128)S(1)}, f32[4,4,1,256]...) custom-call(s32[8]{0:T(128)} %hub_ids.1, ...), custom_call_target="tpu_custom_call" | custom-call | tf_op jit(solution)/shard_map/near/pallas_call | solution.py:258
  44.6 0.0 copy-done.1
  44.6 0.0 copy-done.3
  44.6 0.0 copy-done
  44.6 0.0 copy-done.2
  44.7 0.0 copy-start.5
  44.7 0.0 copy-start.4
  44.7 13.6 %hub.1 = (bf16[1024,256]{1,0:T(8,128)(2,1)S(1)}, f32[4,4,80,256]{3,2,1,0:T(8,128)S(1)}, f32[4,4,1,256]{3,2,1,0:T(1,128)S(1)}) custom-call(s32[8]{0:T(128)S(1)} %copy-done.2, s32[4,16]{1,0:T(4,128)S(1)} %copy-done.1, s32[4]{0:T(128)S(1)} %copy-done.3, ...), custom_call_target="tpu_custom_call", output_to_operand_aliasing={{1}: (5, {}), {2}: (6, {})} | custom-call | tf_op jit(solution)/shard_map/hub/pallas_call | solution.py:356
  58.3 0.2 collective-permute-start
  58.6 0.0 copy-done.5
  58.6 0.3 fusion.2
  58.9 1.4 %collective-permute-done = bf16[1024,256]{1,0:T(8,128)(2,1)S(1)} collective-permute-done((bf16[1024,256]{1,0:T(8,128)(2,1)S(1)}, bf16[1024,256]{1,0:T(8,128)(2,1)S(1)}, u32[]{:S(2)}, u32[]{:S(2)}) %collective-permute-start) | collective-permute-done | bytes 524320 | tf_op jit(solution)/shard_map/ppermute | solution.py:387
  60.3 0.0 copy-done.4
  60.3 1.1 %fusion.1 = bf16[1024,256]{1,0:T(8,128)(2,1)} fusion(f32[1024,256]{1,0:T(8,128)S(1)} %fusion.2, bf16[1024,256]{1,0:T(8,128)(2,1)S(1)} %collective-permute-done, bf16[256,256]{1,0:T(8,128)(2,1)S(1)} %get-tuple-element.22, bf16[1024,512]{1,0:T(8,128)(2,1)S(1)} %copy-done.4, s32[]{:T(128)S(6)} %select_n.4), kind=kOutput, calls=%fused_computation.2 | convolution fusion | flops 135266304 | bytes 2752516 | tf_op jit(solution)/shard_map/dot_general | solution.py:390
Async XLA Ops:
  0.0 44.6 %copy-start.1 = (s32[4,16]{1,0:T(4,128)S(1)}, s32[4,16]{1,0:T(4,128)}, u32[]{:S(2)}) copy-start(s32[4,16]{1,0:T(4,128)} %lists.1) | copy-start | bytes 772
  0.0 44.6 %copy-start.3 = (s32[4]{0:T(128)S(1)}, s32[4]{0:T(128)}, u32[]{:S(2)}) copy-start(s32[4]{0:T(128)} %counts.1) | copy-start | bytes 52
  0.0 44.6 %copy-start = (s32[131072]{0:T(1024)S(1)}, s32[131072]{0:T(1024)}, u32[]{:S(2)}) copy-start(s32[131072]{0:T(1024)} %mask.3) | copy-start | bytes 1572868
  0.0 44.6 %copy-start.2 = (s32[8]{0:T(128)S(1)}, s32[8]{0:T(128)}, u32[]{:S(2)}) copy-start(s32[8]{0:T(128)} %hub_ids.1) | copy-start | bytes 100
  44.7 13.9 %copy-start.5 = (bf16[256,512]{1,0:T(8,128)(2,1)S(1)}, bf16[256,512]{1,0:T(8,128)(2,1)}, u32[]{:S(2)}) copy-start(bf16[256,512]{1,0:T(8,128)(2,1)} %w_out.1) | copy-start | bytes 786436
  44.7 15.7 %copy-start.4 = (bf16[1024,512]{1,0:T(8,128)(2,1)S(1)}, bf16[1024,512]{1,0:T(8,128)(2,1)}, u32[]{:S(2)}) copy-start(bf16[1024,512]{1,0:T(8,128)(2,1)} %param.7) | copy-start | bytes 3145732
  58.3 2.0 %collective-permute-start = (bf16[1024,256]{1,0:T(8,128)(2,1)S(1)}, bf16[1024,256]{1,0:T(8,128)(2,1)S(1)}, u32[]{:S(2)}, u32[]{:S(2)}) collective-permute-start(bf16[1024,256]{1,0:T(8,128)(2,1)S(1)} %get-tuple-element.21), channel_id=1, source_target_pairs={{0,1},{1,0},{2,3},{3,2},{4,5},{5,4},{6,7},{7,6},{8,9},{9,8},{10,11... | collective-permute-start | bytes 1572872 | tf_op jit(solution)/shard_map/ppermute | solution.py:387

commit v7 on v6

--- a/solution.py
+++ b/solution.py
@@ -294,7 +294,7 @@
 
 
 def hub_kernel(hub_ids, lists, counts, hubs, q_t, acc_in, top_in, norm, wk, wv_t, mask, out, acc, top,
-               marks, mark_sem, keys, vals, bias, att_t, cnt):
+               marks, mark_sem, keys, vals, bias, att_t, cnt, named, length):
     loads = []
     for k in range(8):
         loads.append(pltpu.make_async_copy(mask.at[pl.ds(pl.multiple_of(hub_ids[k] * B, B), B)], marks.at[k, 0],
@@ -305,11 +305,16 @@
             cnt[b, i] = 0
         for j in range(1, 5):
             cnt[b, lists[b, j]] += jnp.where(j < counts[b], 1, 0)
+        length[b] = 0
+        for k in range(8):
+            named[b, length[b]] = k
+            length[b] += jnp.where(cnt[b, k] > 0, 1, 0)
+    for copy in loads:
+        copy.wait()
     longest = jnp.zeros((1, 128), F32)
     for k in range(8):
         rows = jnp.concatenate([
             jnp.concatenate([hubs[c, p, k] for p in range(16)], axis=0) for c in range(2)], axis=1)
-        loads[k].wait()
         usable = (marks[k] > 0).astype(F32)
         project(rows, wk[...], wv_t[...], usable, keys, vals, bias, k)
         longest = jnp.maximum(longest, squares(keys[k]))
@@ -330,16 +335,26 @@
 
     @pl.when(close)
     def _():
-        def step(b, k, times):
-            kb = keys[k]
-            scale = times.astype(F32)
+        def step(b, *entries):
+            which = [named[b, e] for e in entries]
+            scales = [cnt[b, k].astype(F32) for k in which]
+            kb = jnp.concatenate([keys[k] for k in which], axis=0)
             ss = [jnp.dot(kb, q_t[b, h], preferred_element_type=F32) for h in heads]
             ps = [jnp.exp(ss[h] - top[b, h]).astype(BF16) for h in heads]
-            got = [jnp.dot(vals[k, h], ps[h], preferred_element_type=F32) for h in heads]
             for h in heads:
-                acc[b, h] += scale * got[h]
-
-        over_hubs(step)
+                acc[b, h] += sum(
+                    scale * jnp.dot(vals[k, h], ps[h][n * B:(n + 1) * B, :], preferred_element_type=F32)
+                    for n, (k, scale) in enumerate(zip(which, scales)))
+
+        @pl.loop(0, 4)
+        def _(b):
+            @pl.loop(0, length[b] // 2)
+            def _(n):
+                step(b, 2 * n, 2 * n + 1)
+
+            @pl.when(length[b] % 2 == 1)
+            def _():
+                step(b, length[b] - 1)
 
     @pl.when(jnp.logical_not(close))
     def _():
@@ -369,6 +384,8 @@
             pltpu.VMEM((8, B, 128), F32),
             pltpu.VMEM((B, B), BF16),
             pltpu.SMEM((4, 8), jnp.int32),
+            pltpu.SMEM((4, 8), jnp.int32),
+            pltpu.SMEM((4,), jnp.int32),
         ],
         compiler_params=pltpu.CompilerParams(vmem_limit_bytes=40 << 20),
         name="hub",

time: 61.5 us -> 60.6 us (0.985)
  the two profiles are of different devices: /device:TPU:3 before, /device:TPU:9 now
where the time goes in v7:
time: 60.6 us; the launch traced here: 59.5 us
  Pallas kernels  56.3 us (93%)
  waiting for transfers between devices  1.47 us (2%)
  matrix products  1.39 us (2%)
    pallas_call x1, Pallas kernels, near_attention(): pl.pallas_call(near_kernel, out_shape=(jax.ShapeDtypeStruct((2, 16, 8, 16...  44.4 us
    pallas_call x1, Pallas kernels, hub_attention(): pl.pallas_call(hub_kernel, out_shape=(jax.ShapeDtypeStruct((1024, 256), B...  11.9 us
    ppermute x1, waiting for transfers between devices, body(): theirs = lax.ppermute(attended, 'head', [(0, 1), (1, 0)])  1.47 us
  transfers between devices with their start and end apart: 1, of which 1 were waited for; matrix products, arithmetic and copies ran while one was open for 0% of the time, Pallas kernels for 0%

profile of v7, /device:TPU:9, one launch (start us, length us, event | category | flops | bytes accessed | tf_op | source)
XLA Modules:
  0.0 59.5 jit_solution(629803214579945243)
XLA Ops:
  0.0 0.0 copy-start.1
  0.0 0.0 copy-start.3
  0.0 0.0 copy-start
  0.0 0.0 copy-start.2
  0.0 44.4 %near.1 = (bf16[2,16,8,16,256]{4,3,2,1,0:T(8,128)(2,1)S(1)}, bf16[4,4,256,256]{3,2,1,0:T(8,128)(2,1)S(1)}, f32[4,4,80,256]{3,2,1,0:T(8,128)S(1)}, f32[4,4,1,256]...) custom-call(s32[8]{0:T(128)} %hub_ids.1, ...), custom_call_target="tpu_custom_call" | custom-call | tf_op jit(solution)/shard_map/near/pallas_call | solution.py:258
  44.5 0.0 copy-done.1
  44.5 0.0 copy-done.3
  44.5 0.0 copy-done
  44.5 0.0 copy-done.2
  44.5 0.0 copy-start.5
  44.5 0.0 copy-start.4
  44.5 11.9 %hub.1 = (bf16[1024,256]{1,0:T(8,128)(2,1)S(1)}, f32[4,4,80,256]{3,2,1,0:T(8,128)S(1)}, f32[4,4,1,256]{3,2,1,0:T(1,128)S(1)}) custom-call(s32[8]{0:T(128)S(1)} %copy-done.2, s32[4,16]{1,0:T(4,128)S(1)} %copy-done.1, s32[4]{0:T(128)S(1)} %copy-done.3, ...), custom_call_target="tpu_custom_call", output_to_operand_aliasing={{1}: (5, {}), {2}: (6, {})} | custom-call | tf_op jit(solution)/shard_map/hub/pallas_call | solution.py:371
  56.4 0.2 collective-permute-start
  56.7 0.0 copy-done.5
  56.7 0.3 fusion.2
  57.0 1.5 %collective-permute-done = bf16[1024,256]{1,0:T(8,128)(2,1)S(1)} collective-permute-done((bf16[1024,256]{1,0:T(8,128)(2,1)S(1)}, bf16[1024,256]{1,0:T(8,128)(2,1)S(1)}, u32[]{:S(2)}, u32[]{:S(2)}) %collective-permute-start) | collective-permute-done | bytes 524320 | tf_op jit(solution)/shard_map/ppermute | solution.py:404
  58.4 0.0 copy-done.4
  58.4 1.1 %fusion.1 = bf16[1024,256]{1,0:T(8,128)(2,1)} fusion(f32[1024,256]{1,0:T(8,128)S(1)} %fusion.2, bf16[1024,256]{1,0:T(8,128)(2,1)S(1)} %collective-permute-done, bf16[256,256]{1,0:T(8,128)(2,1)S(1)} %get-tuple-element.22, bf16[1024,512]{1,0:T(8,128)(2,1)S(1)} %copy-done.4, s32[]{:T(128)S(6)} %select_n.4), kind=kOutput, calls=%fused_computation.2 | convolution fusion | flops 135266304 | bytes 2752516 | tf_op jit(solution)/shard_map/dot_general | solution.py:407
Async XLA Ops:
  0.0 44.5 %copy-start.1 = (s32[4,16]{1,0:T(4,128)S(1)}, s32[4,16]{1,0:T(4,128)}, u32[]{:S(2)}) copy-start(s32[4,16]{1,0:T(4,128)} %lists.1) | copy-start | bytes 772
  0.0 44.5 %copy-start.3 = (s32[4]{0:T(128)S(1)}, s32[4]{0:T(128)}, u32[]{:S(2)}) copy-start(s32[4]{0:T(128)} %counts.1) | copy-start | bytes 52
  0.0 44.5 %copy-start = (s32[131072]{0:T(1024)S(1)}, s32[131072]{0:T(1024)}, u32[]{:S(2)}) copy-start(s32[131072]{0:T(1024)} %mask.3) | copy-start | bytes 1572868
  0.0 44.5 %copy-start.2 = (s32[8]{0:T(128)S(1)}, s32[8]{0:T(128)}, u32[]{:S(2)}) copy-start(s32[8]{0:T(128)} %hub_ids.1) | copy-start | bytes 100
  44.5 12.2 %copy-start.5 = (bf16[256,512]{1,0:T(8,128)(2,1)S(1)}, bf16[256,512]{1,0:T(8,128)(2,1)}, u32[]{:S(2)}) copy-start(bf16[256,512]{1,0:T(8,128)(2,1)} %w_out.1) | copy-start | bytes 786436
  44.5 13.9 %copy-start.4 = (bf16[1024,512]{1,0:T(8,128)(2,1)S(1)}, bf16[1024,512]{1,0:T(8,128)(2,1)}, u32[]{:S(2)}) copy-start(bf16[1024,512]{1,0:T(8,128)(2,1)} %param.7) | copy-start | bytes 3145732
  56.4 2.0 %collective-permute-start = (bf16[1024,256]{1,0:T(8,128)(2,1)S(1)}, bf16[1024,256]{1,0:T(8,128)(2,1)S(1)}, u32[]{:S(2)}, u32[]{:S(2)}) collective-permute-start(bf16[1024,256]{1,0:T(8,128)(2,1)S(1)} %get-tuple-element.21), channel_id=1, source_target_pairs={{0,1},{1,0},{2,3},{3,2},{4,5},{5,4},{6,7},{7,6},{8,9},{9,8},{10,11... | collective-permute-start | bytes 1572872 | tf_op jit(solution)/shard_map/ppermute | solution.py:404

commit v8 on v7

--- a/solution.py
+++ b/solution.py
@@ -360,11 +360,10 @@
     def _():
         over_hubs(lambda b, k, times: attend(q_t, b, keys[k], vals.at[k], bias[k], times, acc, top))
 
-    @pl.loop(0, 4)
-    def _(b):
+    for b in range(4):
         for h in heads:
-            att_t[h * DH:(h + 1) * DH, :] = (acc[b, h, 0:DH, :] * (1.0 / acc[b, h, DH:DH + 1, :])).astype(BF16)
-        out[pl.ds(pl.multiple_of(b * B, B), B), :] = att_t[...].T
+            att_t[b, h * DH:(h + 1) * DH, :] = (acc[b, h, 0:DH, :] * (1.0 / acc[b, h, DH:DH + 1, :])).astype(BF16)
+        out[b * B:(b + 1) * B, :] = att_t[b].T
 
 
 def hub_attention(hub_ids, lists, counts, hubs, q_t, acc, top, norm, wk, wv_t, mask):
@@ -382,7 +381,7 @@
             pltpu.VMEM((8, B, B), BF16),
             pltpu.VMEM((8, HEADS_HERE, TALL, B), BF16),
             pltpu.VMEM((8, B, 128), F32),
-            pltpu.VMEM((B, B), BF16),
+            pltpu.VMEM((4, B, B), BF16),
             pltpu.SMEM((4, 8), jnp.int32),
             pltpu.SMEM((4, 8), jnp.int32),
             pltpu.SMEM((4,), jnp.int32),

time: 60.6 us -> 60.5 us (level)
  the two profiles are of different devices: /device:TPU:9 before, /device:TPU:5 now
where the time goes in v8:
time: 60.5 us; the launch traced here: 60.6 us
  Pallas kernels  57.4 us (95%)
  waiting for transfers between devices  1.45 us (2%)
  matrix products  1.4 us (2%)
    pallas_call x1, Pallas kernels, near_attention(): pl.pallas_call(near_kernel, out_shape=(jax.ShapeDtypeStruct((2, 16, 8, 16...  44.5 us
    pallas_call x1, Pallas kernels, hub_attention(): pl.pallas_call(hub_kernel, out_shape=(jax.ShapeDtypeStruct((1024, 256), B...  13 us
    ppermute x1, waiting for transfers between devices, body(): theirs = lax.ppermute(attended, 'head', [(0, 1), (1, 0)])  1.45 us
  transfers between devices with their start and end apart: 1, of which 1 were waited for; matrix products, arithmetic and copies ran while one was open for 0% of the time, Pallas kernels for 0%

profile of v8, /device:TPU:5, one launch (start us, length us, event | category | flops | bytes accessed | tf_op | source)
XLA Modules:
  0.0 60.6 jit_solution(14746218373605548346)
XLA Ops:
  0.0 0.0 copy-start.1
  0.0 0.0 copy-start.3
  0.0 0.0 copy-start
  0.0 0.0 copy-start.2
  0.0 44.5 %near.1 = (bf16[2,16,8,16,256]{4,3,2,1,0:T(8,128)(2,1)S(1)}, bf16[4,4,256,256]{3,2,1,0:T(8,128)(2,1)S(1)}, f32[4,4,80,256]{3,2,1,0:T(8,128)S(1)}, f32[4,4,1,256]...) custom-call(s32[8]{0:T(128)} %hub_ids.1, ...), custom_call_target="tpu_custom_call" | custom-call | tf_op jit(solution)/shard_map/near/pallas_call | solution.py:258
  44.5 0.0 copy-done.1
  44.5 0.0 copy-done.3
  44.5 0.0 copy-done
  44.5 0.0 copy-done.2
  44.5 0.0 copy-start.5
  44.5 0.0 copy-start.4
  44.5 13.0 %hub.1 = (bf16[1024,256]{1,0:T(8,128)(2,1)S(1)}, f32[4,4,80,256]{3,2,1,0:T(8,128)S(1)}, f32[4,4,1,256]{3,2,1,0:T(1,128)S(1)}) custom-call(s32[8]{0:T(128)S(1)} %copy-done.2, s32[4,16]{1,0:T(4,128)S(1)} %copy-done.1, s32[4]{0:T(128)S(1)} %copy-done.3, ...), custom_call_target="tpu_custom_call", output_to_operand_aliasing={{1}: (5, {}), {2}: (6, {})} | custom-call | tf_op jit(solution)/shard_map/hub/pallas_call | solution.py:370
  57.5 0.2 collective-permute-start
  57.8 0.0 copy-done.5
  57.8 0.3 fusion.2
  58.1 1.5 %collective-permute-done = bf16[1024,256]{1,0:T(8,128)(2,1)S(1)} collective-permute-done((bf16[1024,256]{1,0:T(8,128)(2,1)S(1)}, bf16[1024,256]{1,0:T(8,128)(2,1)S(1)}, u32[]{:S(2)}, u32[]{:S(2)}) %collective-permute-start) | collective-permute-done | bytes 524320 | tf_op jit(solution)/shard_map/ppermute | solution.py:403
  59.5 0.0 copy-done.4
  59.5 1.1 %fusion.1 = bf16[1024,256]{1,0:T(8,128)(2,1)} fusion(f32[1024,256]{1,0:T(8,128)S(1)} %fusion.2, bf16[1024,256]{1,0:T(8,128)(2,1)S(1)} %collective-permute-done, bf16[256,256]{1,0:T(8,128)(2,1)S(1)} %get-tuple-element.22, bf16[1024,512]{1,0:T(8,128)(2,1)S(1)} %copy-done.4, s32[]{:T(128)S(6)} %select_n.4), kind=kOutput, calls=%fused_computation.2 | convolution fusion | flops 135266304 | bytes 2752516 | tf_op jit(solution)/shard_map/dot_general | solution.py:406
Async XLA Ops:
  0.0 44.5 %copy-start.1 = (s32[4,16]{1,0:T(4,128)S(1)}, s32[4,16]{1,0:T(4,128)}, u32[]{:S(2)}) copy-start(s32[4,16]{1,0:T(4,128)} %lists.1) | copy-start | bytes 772
  0.0 44.5 %copy-start.3 = (s32[4]{0:T(128)S(1)}, s32[4]{0:T(128)}, u32[]{:S(2)}) copy-start(s32[4]{0:T(128)} %counts.1) | copy-start | bytes 52
  0.0 44.5 %copy-start = (s32[131072]{0:T(1024)S(1)}, s32[131072]{0:T(1024)}, u32[]{:S(2)}) copy-start(s32[131072]{0:T(1024)} %mask.3) | copy-start | bytes 1572868
  0.0 44.5 %copy-start.2 = (s32[8]{0:T(128)S(1)}, s32[8]{0:T(128)}, u32[]{:S(2)}) copy-start(s32[8]{0:T(128)} %hub_ids.1) | copy-start | bytes 100
  44.5 13.2 %copy-start.5 = (bf16[256,512]{1,0:T(8,128)(2,1)S(1)}, bf16[256,512]{1,0:T(8,128)(2,1)}, u32[]{:S(2)}) copy-start(bf16[256,512]{1,0:T(8,128)(2,1)} %w_out.1) | copy-start | bytes 786436
  44.5 15.0 %copy-start.4 = (bf16[1024,512]{1,0:T(8,128)(2,1)S(1)}, bf16[1024,512]{1,0:T(8,128)(2,1)}, u32[]{:S(2)}) copy-start(bf16[1024,512]{1,0:T(8,128)(2,1)} %param.7) | copy-start | bytes 3145732
  57.5 2.0 %collective-permute-start = (bf16[1024,256]{1,0:T(8,128)(2,1)S(1)}, bf16[1024,256]{1,0:T(8,128)(2,1)S(1)}, u32[]{:S(2)}, u32[]{:S(2)}) collective-permute-start(bf16[1024,256]{1,0:T(8,128)(2,1)S(1)} %get-tuple-element.21), channel_id=1, source_target_pairs={{0,1},{1,0},{2,3},{3,2},{4,5},{5,4},{6,7},{7,6},{8,9},{9,8},{10,11... | collective-permute-start | bytes 1572872 | tf_op jit(solution)/shard_map/ppermute | solution.py:403
